TPU v7x, 128 devices: a whole 4x4x4 slice. The times are simulated.
128 devices in a mesh: dom: 8 (over y, core), spec: 16 (over x, z).
Axes of the slice: x: 4, y: 4, z: 4, core: 2. Of those that a mesh axis runs over, the one named last changes fastest.
Arguments:
- spectrum: float32 [256, 524288], P('spec', 'dom'), may hold values from -6 to 6
- conductance: float32 [256, 524288], P(None, ('dom', 'spec')), may hold values from 0.05 to 2
- capacitance: float32 [256, 524288], P(None, ('dom', 'spec')), may hold values from 0.05 to 2
- block_cond: float32 [4096, 128, 128], P(('dom', 'spec')), may hold values from -0.5 to 0.5
- block_cap: float32 [4096, 128, 128], P(('dom', 'spec')), may hold values from -0.5 to 0.5
- boundary_nodes: int32 [8, 256], P('dom'), may hold values from 0 to 65535, as said below
- couple_src: int32 [8, 7], P('dom'), may hold values from 0 to 7, as said below
- couple_count: int32 [8], P('dom'), may hold values from 1 to 7, as said below
- couple_cond: float32 [8, 7, 256, 256], P('dom'), may hold values from -0.375 to 0.375
- couple_cap: float32 [8, 7, 256, 256], P('dom'), may hold values from -0.375 to 0.375
Outputs:
- jacobian_product: float32 [256, 524288], P('spec', 'dom')
Inputs may be any that keep to these rules, and one draw needn't show every extreme that they name: `boundary_nodes`: row d lists 256 distinct nodes of partition d; entries 16 * s to 16 * (s + 1) - 1 lie among nodes 4096 * s to 4096 * (s + 1) - 1 and increase. `couple_src`: row d holds every partition other than d once. Partition d uses the first couple_count[d] entries of its rows of couple_src, couple_cond and couple_cap; some partition uses all 7.
All inputs are finite; a program needn't handle non-finite values.
Results may differ from a plain program's by a relative error of at most 0.0001.
Values sent between devices are 32-bit elements; how exact they have to be, the bound alone decides.
No kernel may reach another device: no remote copies, remote signals or barrier semaphores. Data moves between devices by JAX's collectives and lax.ppermute only.
A program may use at most 192 MiB of HBM per device.

v0:
```python
import functools
import math

import jax
import jax.numpy as jnp
import numpy as np
from jax import lax
from jax.experimental import pallas as pl
from jax.experimental.pallas import tpu as pltpu
from jax.sharding import PartitionSpec as P

F32 = jnp.float32
BF16 = jnp.bfloat16
PARTS = 2
TILE = 512


def fourier_tables(length):
    harmonic = np.arange(length) // 2
    harmonic[1] = length // 2
    phase = np.arange(length)[:, None] * harmonic[None, :] % length
    angles = phase * (2.0 * math.pi / length)
    is_sine = (np.arange(length) % 2 == 1) & (np.arange(length) >= 2)
    basis = np.where(is_sine[None, :], np.sin(angles), np.cos(angles))
    scale = np.where(np.arange(length) < 2, 1.0 / length, 2.0 / length)
    return basis.astype(np.float32), (basis.T * scale[:, None]).astype(np.float32)


def widened(table):
    high = table.astype(jnp.bfloat16)
    low = (table - high.astype(np.float32)).astype(jnp.bfloat16)
    return jnp.asarray(np.concatenate([high, high, low], axis=1))


def halves(x):
    high = x.astype(BF16)
    return high, (x - high.astype(F32)).astype(BF16)


def derive(x, first_row, length):
    rows = lax.broadcasted_iota(jnp.int32, x.shape, 0)
    up = pltpu.roll(x, x.shape[0] - 1, 0)
    down = pltpu.roll(x, 1, 0)
    freq = ((rows + first_row) // 2).astype(F32) * (2.0 / length)
    return freq * jnp.where(rows % 2 == 0, up, -down)


def nodal_kernel(length, block, s_ref, g_ref, c_ref, cond_ref, cap_ref, basis_ref, forward_ref, o_ref):
    s_high, s_low = halves(s_ref[...])
    waves = jnp.dot(
        basis_ref[...],
        jnp.concatenate([s_high, s_low, s_high], axis=0),
        preferred_element_type=F32,
    )

    def onward(values):
        high, low = halves(values)
        return jnp.dot(
            forward_ref[...],
            jnp.concatenate([high, low, high], axis=0),
            preferred_element_type=F32,
        )

    direct = onward(g_ref[...] * waves)
    stored = onward(c_ref[...] * waves)
    direct_net = []
    stored_net = []
    for b in range(cond_ref.shape[0]):
        cond_high, cond_low = halves(cond_ref[b])
        cap_high, cap_low = halves(cap_ref[b])
        left = jnp.concatenate(
            [
                s_high[:, b * block : (b + 1) * block],
                s_low[:, b * block : (b + 1) * block],
                s_high[:, b * block : (b + 1) * block],
            ],
            axis=1,
        )
        right = jnp.concatenate(
            [
                jnp.concatenate([cond_high, cond_high, cond_low], axis=1),
                jnp.concatenate([cap_high, cap_high, cap_low], axis=1),
            ],
            axis=0,
        )
        both = lax.dot_general(
            left, right, (((1,), (1,)), ((), ())), preferred_element_type=F32
        )
        direct_net.append(both[:, :block])
        stored_net.append(both[:, block:])
    direct = direct + jnp.concatenate(direct_net, axis=1)
    stored = stored + jnp.concatenate(stored_net, axis=1)
    o_ref[...] = direct + derive(stored, 0, length)


def nodal(part, s, conductance, capacitance, block_cond, block_cap, basis, forward):
    length, width = s.shape
    block = block_cond.shape[1]
    steps = width // TILE
    per = TILE // block
    column = lambda i: (0, part * steps + i)
    blocks = pl.BlockSpec((per, block, block), lambda i: (part * steps + i, 0, 0))
    table = pl.BlockSpec((length, 3 * length), lambda i: (0, 0))
    return pl.pallas_call(
        functools.partial(nodal_kernel, length, block),
        grid=(steps,),
        in_specs=[
            pl.BlockSpec((length, TILE), lambda i: (0, i)),
            pl.BlockSpec((length, TILE), column),
            pl.BlockSpec((length, TILE), column),
            blocks,
            blocks,
            table,
            table,
        ],
        out_specs=pl.BlockSpec((length, TILE), lambda i: (0, i)),
        out_shape=jax.ShapeDtypeStruct(s.shape, F32),
        compiler_params=pltpu.CompilerParams(vmem_limit_bytes=48 << 20),
        cost_estimate=pl.CostEstimate(
            flops=24 * length * length * width, transcendentals=0, bytes_accessed=20 * length * width
        ),
        name="nodal",
    )(s, conductance, capacitance, block_cond, block_cap, basis, forward)


def pack_kernel(offset, stride, x_ref, o_ref, sem):
    count, _, width = o_ref.shape
    copies = [
        pltpu.make_async_copy(
            x_ref.at[:, pl.ds(t * stride + offset, width)], o_ref.at[t], sem.at[t]
        )
        for t in range(count)
    ]
    for copy in copies:
        copy.start()
    for copy in copies:
        copy.wait()


def pack(x, part, count):
    rows, columns = x.shape
    stride = columns // count
    width = stride // PARTS
    return pl.pallas_call(
        functools.partial(pack_kernel, part * width, stride),
        in_specs=[pl.BlockSpec(memory_space=pl.ANY)],
        out_specs=pl.BlockSpec(memory_space=pl.ANY),
        out_shape=jax.ShapeDtypeStruct((count, rows, width), F32),
        scratch_shapes=[pltpu.SemaphoreType.DMA((count,))],
        name="pack",
    )(x)


def pick_kernel(per, nodes_ref, x_ref, o_ref):
    t = pl.program_id(0)
    width = x_ref.shape[1]
    lanes = lax.broadcasted_iota(jnp.int32, (x_ref.shape[0], 128), 1)
    total = jnp.zeros((x_ref.shape[0], 128), F32)
    for j in range(per):
        place = jnp.clip(nodes_ref[t * per + j] - t * width, 0, width - 1)
        tile = x_ref[:, pl.ds(pl.multiple_of(place // 128 * 128, 128), 128)]
        turned = pltpu.roll(tile, (j - place % 128 + 128) % 128, 1)
        total = jnp.where(lanes == j, turned, total)
    o_ref[...] = total


def pick(x, nodes, count):
    rows, columns = x.shape
    per = nodes.shape[0] // count
    picked = pl.pallas_call(
        functools.partial(pick_kernel, per),
        grid_spec=pltpu.PrefetchScalarGridSpec(
            num_scalar_prefetch=1,
            grid=(count,),
            in_specs=[pl.BlockSpec((rows, columns // count), lambda t, n: (0, t))],
            out_specs=pl.BlockSpec((None, rows, 128), lambda t, n: (t, 0, 0)),
        ),
        out_shape=jax.ShapeDtypeStruct((count, rows, 128), F32),
        name="pick",
    )(nodes, x)
    return picked[:, :, :per].transpose(1, 0, 2).reshape(rows, nodes.shape[0])


def couple_kernel(length, scalars_ref, x_ref, cond_ref, cap_ref, o_ref):
    c = pl.program_id(0)

    @pl.when(c == 0)
    def _():
        o_ref[...] = jnp.zeros_like(o_ref)

    @pl.when(c < scalars_ref[0])
    def _():
        x = x_ref[...]
        slope = derive(x, scalars_ref[1], length)

        def times(left, right):
            left_high, left_low = halves(left)
            right_high, right_low = halves(right)
            contract = (((1,), (1,)), ((), ()))
            product = functools.partial(
                lax.dot_general, dimension_numbers=contract, preferred_element_type=F32
            )
            return (
                product(left_high, right_high)
                + product(left_low, right_high)
                + product(left_high, right_low)
            )

        o_ref[...] += times(x, cond_ref[...]) + times(slope, cap_ref[...])


def couple(gathered, sources, used, first_row, length, couple_cond, couple_cap):
    _, rows, bound = gathered.shape
    slots = sources.shape[0]
    scalars = jnp.concatenate([used, first_row[None], sources])
    table = pl.BlockSpec((None, None, bound, bound), lambda c, n: (0, c, 0, 0))
    return pl.pallas_call(
        functools.partial(couple_kernel, length),
        grid_spec=pltpu.PrefetchScalarGridSpec(
            num_scalar_prefetch=1,
            grid=(slots,),
            in_specs=[
                pl.BlockSpec((None, rows, bound), lambda c, n: (n[2 + c], 0, 0)),
                table,
                table,
            ],
            out_specs=pl.BlockSpec((rows, bound), lambda c, n: (0, 0)),
        ),
        out_shape=jax.ShapeDtypeStruct((rows, bound), F32),
        name="couple",
    )(scalars, gathered, couple_cond, couple_cap)


def place_kernel(part, stride, group, nodes_ref, y_ref, extra_ref, *rest):
    o_ref = rest[-1]
    step = pl.program_id(0)
    _, rows, width = y_ref.shape
    per = extra_ref.shape[2]
    lanes = lax.broadcasted_iota(jnp.int32, (rows, 128), 1)
    for g in range(group):
        t = step * group + g
        lo = g * stride + part * width
        o_ref[:, g * width : (g + 1) * width] = y_ref[g]
        extra = extra_ref[g]
        for j in range(per):
            local = nodes_ref[t * per + j] - t * stride - part * width
            first = jnp.clip(local // 128, 0, width // 128 - 1) * 128
            at = pl.ds(pl.multiple_of(g * width + first, 128), 128)
            old = o_ref[:, at]
            o_ref[:, at] = old + jnp.where(lanes + first == local, extra[:, j : j + 1], 0.0)


def place(y, extra, nodes, part, held):
    count, rows, width = y.shape
    per = nodes.shape[0] // count
    stride = width * PARTS
    in_specs = [
        pl.BlockSpec((1, rows, width), lambda t, n: (t, 0, 0)),
        pl.BlockSpec((1, rows, per), lambda t, n: (t, 0, 0)),
    ]
    args = [y, extra]
    aliases = {}
    if held is not None:
        in_specs.append(pl.BlockSpec(memory_space=pl.ANY))
        args.append(held)
        aliases = {3: 0}
    return pl.pallas_call(
        functools.partial(place_kernel, part, stride, 1),
        grid_spec=pltpu.PrefetchScalarGridSpec(
            num_scalar_prefetch=1,
            grid=(count,),
            in_specs=in_specs,
            out_specs=pl.BlockSpec((rows, width), lambda t, n: (0, t * PARTS + part)),
        ),
        out_shape=jax.ShapeDtypeStruct((rows, count * stride), F32),
        input_output_aliases=aliases,
        name="place",
    )(nodes, *args)


def shards(
    spectrum,
    conductance,
    capacitance,
    block_cond,
    block_cap,
    boundary_nodes,
    couple_src,
    couple_count,
    couple_cond,
    couple_cap,
):
    length = conductance.shape[0]
    rows = spectrum.shape[0]
    count = lax.axis_size("spec")
    basis_table, forward_table = fourier_tables(length)
    basis, forward = widened(basis_table), widened(forward_table)
    nodes = boundary_nodes[0]
    nodal_args = (conductance, capacitance, block_cond, block_cap, basis, forward)

    def swap(x):
        return lax.all_to_all(x, "spec", split_axis=0, concat_axis=0, tiled=True)

    arrived = []
    for part in range(PARTS):
        got = swap(pack(spectrum, part, count))
        arrived.append(got.reshape(length, got.shape[2]))

    own_boundary = pick(spectrum, nodes, count)
    gathered = lax.all_gather(own_boundary, "dom", axis=0, tiled=False)
    extra = couple(
        gathered,
        couple_src[0],
        couple_count,
        lax.axis_index("spec") * rows,
        length,
        couple_cond,
        couple_cap,
    )
    extra = extra.reshape(rows, count, nodes.shape[0] // count).transpose(1, 0, 2)

    result = None
    for part in range(PARTS):
        current = nodal(part, arrived[part], *nodal_args)
        back = swap(current.reshape(count, rows, current.shape[1]))
        result = place(back, extra, nodes, part, result)
    return result


def solution(mesh):
    return jax.shard_map(
        shards,
        mesh=mesh,
        in_specs=(
            P("spec", "dom"),
            P(None, ("dom", "spec")),
            P(None, ("dom", "spec")),
            P(("dom", "spec"), None, None),
            P(("dom", "spec"), None, None),
            P("dom", None),
            P("dom", None),
            P("dom"),
            P("dom", None, None, None),
            P("dom", None, None, None),
        ),
        out_specs=P("spec", "dom"),
        check_vma=False,
    )
```

profile of v0, /device:TPU:0, one launch (start us, length us, event | category | flops | bytes accessed | tf_op | source)
XLA Modules:
  0.0 271.6 jit_solution(6860900887599399565)
XLA Ops:
  0.0 64.8 %pack.3 = f32[16,16,2048]{2,1,0:T(8,128)} custom-call(f32[16,65536]{1,0:T(8,128)} %x_ref.5), custom_call_target="tpu_custom_call" | custom-call | tf_op jit(solution)/shard_map/pack/pallas_call | solution.py:144
  64.8 8.0 %all-to-all-start.2 = ((f32[16,16,2048]{2,1,0:T(8,128)}), f32[16,16,2048]{2,1,0:T(8,128)S(1)}, u32[]{:S(2)}, u32[]{:S(2)}) async-start(f32[16,16,2048]{2,1,0:T(8,128)} %pack.3), calls=%async_computation.2 | async-start | bytes 4194304 | tf_op jit(solution)/shard_map/all_to_all | solution.py:302
  72.8 64.8 %pack.2 = f32[16,16,2048]{2,1,0:T(8,128)} custom-call(f32[16,65536]{1,0:T(8,128)} %x_ref.5), custom_call_target="tpu_custom_call" | custom-call | tf_op jit(solution)/shard_map/pack/pallas_call | solution.py:144
  137.5 0.0 copy-start.3
  137.6 0.0 copy-start.4
  137.6 0.0 all-to-all-done.2
  137.6 0.0 copy-start
  137.6 1.3 copy-done
  138.9 7.2 %all-to-all-start = ((f32[16,16,2048]{2,1,0:T(8,128)}), f32[16,16,2048]{2,1,0:T(8,128)S(1)}, u32[]{:S(2)}, u32[]{:S(2)}) async-start(f32[16,16,2048]{2,1,0:T(8,128)} %pack.2), calls=%async_computation | async-start | bytes 4194304 | tf_op jit(solution)/shard_map/all_to_all | solution.py:302
  146.1 0.0 copy-done.3
  146.2 0.0 copy-done.4
  146.2 0.0 copy-start.1
  146.2 1.6 copy-done.1
  147.8 6.5 %nodal.3 = f32[256,2048]{1,0:T(8,128)S(1)} custom-call(f32[256,2048]{1,0:T(8,128)S(1)} %bitcast.13, f32[256,4096]{1,0:T(8,128)} %g_ref.3, f32[256,4096]{1,0:T(8,128)} %c_ref.3, f32[32,128,128]{2,1,0:T(8,128)} %cond_ref.5, f32[32,128,128]{2,1,0:T(8,128)} %cap_ref.5, bf16[256,768]{1,0:T(8,128)(2,1)S(1)} %copy-done.4, bf16[256,768]{1,0:T(8,128)(2,1)S(1)} %copy-done.3), custom_call_target="tpu_custom_call" | custom-call | flops 3221225472 | bytes 10485760 | tf_op jit(solution)/shard_map/nodal/pallas_call | solution.py:104
  154.3 0.0 copy-start.2
  154.3 1.3 copy-done.2
  155.6 19.7 %all-to-all-done = f32[16,16,2048]{2,1,0:T(8,128)S(1)} async-done(((f32[16,16,2048]{2,1,0:T(8,128)}), f32[16,16,2048]{2,1,0:T(8,128)S(1)}, u32[]{:S(2)}, u32[]{:S(2)}) %all-to-all-start) | async-done | bytes 2097184 | tf_op jit(solution)/shard_map/all_to_all | solution.py:302
  175.4 4.4 %all-to-all-start.3 = ((f32[16,16,2048]{2,1,0:T(8,128)}), f32[16,16,2048]{2,1,0:T(8,128)}, u32[]{:S(2)}, u32[]{:S(2)}) async-start(f32[16,16,2048]{2,1,0:T(8,128)} %bitcast.14), calls=%async_computation.3 | async-start | bytes 4194304 | tf_op jit(solution)/shard_map/all_to_all | solution.py:302
  179.8 7.5 %nodal.2 = f32[256,2048]{1,0:T(8,128)} custom-call(f32[256,2048]{1,0:T(8,128)S(1)} %bitcast.12, f32[256,4096]{1,0:T(8,128)} %g_ref.3, f32[256,4096]{1,0:T(8,128)} %c_ref.3, f32[32,128,128]{2,1,0:T(8,128)} %cond_ref.5, f32[32,128,128]{2,1,0:T(8,128)} %cap_ref.5, bf16[256,768]{1,0:T(8,128)(2,1)S(1)} %copy-done.4, bf16[256,768]{1,0:T(8,128)(2,1)S(1)} %copy-done.3), custom_call_target="tpu_custom_call" | custom-call | flops 3221225472 | bytes 10485760 | tf_op jit(solution)/shard_map/nodal/pallas_call | solution.py:104
  187.3 19.5 %all-to-all-done.3.y_ref = f32[16,16,2048]{2,1,0:T(8,128)} async-done(((f32[16,16,2048]{2,1,0:T(8,128)}), f32[16,16,2048]{2,1,0:T(8,128)}, u32[]{:S(2)}, u32[]{:S(2)}) %all-to-all-start.3) | async-done | bytes 2097184 | tf_op jit(solution)/shard_map/all_to_all | solution.py:302
  206.9 4.9 %all-to-all-start.1 = ((f32[16,16,2048]{2,1,0:T(8,128)}), f32[16,16,2048]{2,1,0:T(8,128)S(1)}, u32[]{:S(2)}, u32[]{:S(2)}) async-start(f32[16,16,2048]{2,1,0:T(8,128)} %bitcast.2), calls=%async_computation.1 | async-start | bytes 4194304 | tf_op jit(solution)/shard_map/all_to_all | solution.py:302
  212.4 0.0 copy-start.6
  212.4 11.3 %pick.1 = f32[16,16,128]{2,1,0:T(8,128)} custom-call(s32[256]{0:T(256)} %bitcast.17, f32[16,65536]{1,0:T(8,128)} %x_ref.5), custom_call_target="tpu_custom_call" | custom-call | tf_op jit(solution)/shard_map/pick/pallas_call | solution.py:170
  223.7 0.9 slice_bitcast_fusion
  224.7 0.1 all_gather_reshape.3
  224.8 14.3 %all_gather.3.x_ref = f32[8,16,256]{2,1,0:T(8,128)} all-gather(f32[1,16,256]{2,1,0:T(8,128)S(1)} %all_gather_reshape.3), channel_id=1, replica_groups=mesh['dom'=8,'spec'=16] {'dom'}, dimensions={0}, use_global_device_ids=true | all-gather | bytes 147456 | tf_op jit(solution)/shard_map/all_gather | solution.py:310
  239.1 0.0 copy-done.6
  239.1 0.7 pad_add_fusion.scalars_ref
  239.8 6.7 %couple.1 = f32[16,256]{1,0:T(8,128)} custom-call(s32[9]{0:T(128)} %pad_add_fusion.scalars_ref, f32[8,16,256]{2,1,0:T(8,128)} %all_gather.3.x_ref, f32[1,7,256,256]{3,2,1,0:T(8,128)} %cond_ref.4, f32[1,7,256,256]{3,2,1,0:T(8,128)} %cap_ref.4), custom_call_target="tpu_custom_call" | custom-call | tf_op jit(solution)/shard_map/couple/pallas_call | solution.py:217
  246.5 0.8 reshape.17
  247.3 0.7 copy.21
  248.0 11.1 %place.2.rest_0_ = f32[16,65536]{1,0:T(8,128)} custom-call(s32[256]{0:T(256)} %bitcast.18, f32[16,16,2048]{2,1,0:T(8,128)} %all-to-all-done.3.y_ref, f32[16,16,16]{2,1,0:T(8,128)} %bitcast.15), custom_call_target="tpu_custom_call" | custom-call | tf_op jit(solution)/shard_map/place/pallas_call | solution.py:267
  259.1 0.0 all-to-all-done.1.y_ref
  259.1 0.0 copy-start.5
  259.2 1.3 copy-done.5
  260.5 11.1 %place.3 = f32[16,65536]{1,0:T(8,128)} custom-call(s32[256]{0:T(256)} %bitcast.19, f32[16,16,2048]{2,1,0:T(8,128)} %copy-done.5, f32[16,16,16]{2,1,0:T(8,128)} %bitcast.16, f32[16,65536]{1,0:T(8,128)} %place.2.rest_0_), custom_call_target="tpu_custom_call", output_to_operand_aliasing={{}: (3, {})} | custom-call | tf_op jit(solution)/shard_map/place/pallas_call | solution.py:267
  (1 shorter events, 0.0 us)
Async XLA Ops:
  64.8 72.8 %all-to-all-start.2 = ((f32[16,16,2048]{2,1,0:T(8,128)}), f32[16,16,2048]{2,1,0:T(8,128)S(1)}, u32[]{:S(2)}, u32[]{:S(2)}) async-start(f32[16,16,2048]{2,1,0:T(8,128)} %pack.3), calls=%async_computation.2 | async-start | bytes 4194304 | tf_op jit(solution)/shard_map/all_to_all | solution.py:302
  137.5 8.6 %copy-start.3 = (bf16[256,768]{1,0:T(8,128)(2,1)S(1)}, bf16[256,768]{1,0:T(8,128)(2,1)}, u32[]{:S(2)}) copy-start(bf16[256,768]{1,0:T(8,128)(2,1)} %constant.11.clone.forward_ref) | copy-start | bytes 1179652
  137.6 8.6 %copy-start.4 = (bf16[256,768]{1,0:T(8,128)(2,1)S(1)}, bf16[256,768]{1,0:T(8,128)(2,1)}, u32[]{:S(2)}) copy-start(bf16[256,768]{1,0:T(8,128)(2,1)} %constant.10.clone.basis_ref) | copy-start | bytes 1179652
  137.6 1.3 copy-start
  138.9 36.5 %all-to-all-start = ((f32[16,16,2048]{2,1,0:T(8,128)}), f32[16,16,2048]{2,1,0:T(8,128)S(1)}, u32[]{:S(2)}, u32[]{:S(2)}) async-start(f32[16,16,2048]{2,1,0:T(8,128)} %pack.2), calls=%async_computation | async-start | bytes 4194304 | tf_op jit(solution)/shard_map/all_to_all | solution.py:302
  146.2 1.6 copy-start.1
  154.3 1.3 copy-start.2
  175.4 31.5 %all-to-all-start.3 = ((f32[16,16,2048]{2,1,0:T(8,128)}), f32[16,16,2048]{2,1,0:T(8,128)}, u32[]{:S(2)}, u32[]{:S(2)}) async-start(f32[16,16,2048]{2,1,0:T(8,128)} %bitcast.14), calls=%async_computation.3 | async-start | bytes 4194304 | tf_op jit(solution)/shard_map/all_to_all | solution.py:302
  206.9 52.3 %all-to-all-start.1 = ((f32[16,16,2048]{2,1,0:T(8,128)}), f32[16,16,2048]{2,1,0:T(8,128)S(1)}, u32[]{:S(2)}, u32[]{:S(2)}) async-start(f32[16,16,2048]{2,1,0:T(8,128)} %bitcast.2), calls=%async_computation.1 | async-start | bytes 4194304 | tf_op jit(solution)/shard_map/all_to_all | solution.py:302
  212.4 26.8 %copy-start.6 = (s32[1,7]{1,0:T(1,128)S(1)}, s32[1,7]{1,0:T(1,128)}, u32[]{:S(2)}) copy-start(s32[1,7]{1,0:T(1,128)} %param.18) | copy-start | bytes 88
  259.1 1.3 copy-start.5
where the time goes:
time: 274 us; the launch traced here: 272 us
  Pallas kernels  184 us (67%)
  waiting for transfers between devices  39.3 us (14%)
  starting transfers between devices  24.5 us (9%)
  blocking collectives  14.3 us (5%)
  local copies, waits for them, and re-layouts  8.18 us (3%)
    pallas_call x2, Pallas kernels, pack(): pl.pallas_call(functools.partial(pack_kernel, part * width, stride), in_s...  130 us
    all_to_all x4, waiting for transfers between devices, swap(): return lax.all_to_all(x, 'spec', split_axis=0, concat_axis=0, tiled=True)  39.3 us
    all_to_all x4, starting transfers between devices, swap(): return lax.all_to_all(x, 'spec', split_axis=0, concat_axis=0, tiled=True)  24.5 us
    pallas_call x2, Pallas kernels, place(): pl.pallas_call(functools.partial(place_kernel, part, stride, 1), grid_spe...  22.2 us
    all_gather x1, blocking collectives, shards(): gathered = lax.all_gather(own_boundary, 'dom', axis=0, tiled=False)  14.3 us
    pallas_call x2, Pallas kernels, nodal(): pl.pallas_call(functools.partial(nodal_kernel, length, block), grid=(step...  14 us
    pallas_call x1, Pallas kernels, pick(): pl.pallas_call(functools.partial(pick_kernel, per), grid_spec=pltpu.Prefe...  11.3 us
    pallas_call x1, Pallas kernels, couple(): pl.pallas_call(functools.partial(couple_kernel, length), grid_spec=pltpu....  6.71 us
  transfers between devices with their start and end apart: 4, of which 2 were waited for; matrix products, arithmetic and copies ran while one was open for 1% of the time, Pallas kernels for 40%

commit v1 on v0

--- a/solution.py
+++ b/solution.py
@@ -46,7 +46,7 @@
 
 
 def nodal_kernel(length, block, s_ref, g_ref, c_ref, cond_ref, cap_ref, basis_ref, forward_ref, o_ref):
-    s_high, s_low = halves(s_ref[...])
+    s_high, s_low = halves(s_ref[...].reshape(length, s_ref.shape[2]))
     waves = jnp.dot(
         basis_ref[...],
         jnp.concatenate([s_high, s_low, s_high], axis=0),
@@ -90,11 +90,12 @@
         stored_net.append(both[:, block:])
     direct = direct + jnp.concatenate(direct_net, axis=1)
     stored = stored + jnp.concatenate(stored_net, axis=1)
-    o_ref[...] = direct + derive(stored, 0, length)
+    o_ref[...] = (direct + derive(stored, 0, length)).reshape(o_ref.shape)
 
 
 def nodal(part, s, conductance, capacitance, block_cond, block_cap, basis, forward):
-    length, width = s.shape
+    count, rows, width = s.shape
+    length = count * rows
     block = block_cond.shape[1]
     steps = width // TILE
     per = TILE // block
@@ -105,7 +106,7 @@
         functools.partial(nodal_kernel, length, block),
         grid=(steps,),
         in_specs=[
-            pl.BlockSpec((length, TILE), lambda i: (0, i)),
+            pl.BlockSpec((count, rows, TILE), lambda i: (0, 0, i)),
             pl.BlockSpec((length, TILE), column),
             pl.BlockSpec((length, TILE), column),
             blocks,
@@ -113,28 +114,34 @@
             table,
             table,
         ],
-        out_specs=pl.BlockSpec((length, TILE), lambda i: (0, i)),
+        out_specs=pl.BlockSpec((count, rows, TILE), lambda i: (0, 0, i)),
         out_shape=jax.ShapeDtypeStruct(s.shape, F32),
         compiler_params=pltpu.CompilerParams(vmem_limit_bytes=48 << 20),
         cost_estimate=pl.CostEstimate(
             flops=24 * length * length * width, transcendentals=0, bytes_accessed=20 * length * width
         ),
         name="nodal",
-    )(s, conductance, capacitance, block_cond, block_cap, basis, forward)
-
-
-def pack_kernel(offset, stride, x_ref, o_ref, sem):
+    )(in_hbm(s), conductance, capacitance, block_cond, block_cap, basis, forward)
+
+
+def pack_kernel(offset, stride, x_ref, o_ref, held, sem_in, sem_out):
     count, _, width = o_ref.shape
-    copies = [
+    loads = [
         pltpu.make_async_copy(
-            x_ref.at[:, pl.ds(t * stride + offset, width)], o_ref.at[t], sem.at[t]
+            x_ref.at[:, pl.ds(t * stride + offset, width)], held.at[t], sem_in.at[t]
         )
         for t in range(count)
     ]
-    for copy in copies:
-        copy.start()
-    for copy in copies:
-        copy.wait()
+    stores = [
+        pltpu.make_async_copy(held.at[t], o_ref.at[t], sem_out.at[t]) for t in range(count)
+    ]
+    for load in loads:
+        load.start()
+    for load, store in zip(loads, stores):
+        load.wait()
+        store.start()
+    for store in stores:
+        store.wait()
 
 
 def pack(x, part, count):
@@ -146,20 +153,23 @@
         in_specs=[pl.BlockSpec(memory_space=pl.ANY)],
         out_specs=pl.BlockSpec(memory_space=pl.ANY),
         out_shape=jax.ShapeDtypeStruct((count, rows, width), F32),
-        scratch_shapes=[pltpu.SemaphoreType.DMA((count,))],
+        scratch_shapes=[
+            pltpu.VMEM((count, rows, width), F32),
+            pltpu.SemaphoreType.DMA((count,)),
+            pltpu.SemaphoreType.DMA((count,)),
+        ],
         name="pack",
     )(x)
 
 
 def pick_kernel(per, nodes_ref, x_ref, o_ref):
     t = pl.program_id(0)
-    width = x_ref.shape[1]
     lanes = lax.broadcasted_iota(jnp.int32, (x_ref.shape[0], 128), 1)
     total = jnp.zeros((x_ref.shape[0], 128), F32)
     for j in range(per):
-        place = jnp.clip(nodes_ref[t * per + j] - t * width, 0, width - 1)
-        tile = x_ref[:, pl.ds(pl.multiple_of(place // 128 * 128, 128), 128)]
-        turned = pltpu.roll(tile, (j - place % 128 + 128) % 128, 1)
+        spot = nodes_ref[t * per + j]
+        tile = x_ref[:, pl.ds(pl.multiple_of(spot & ~127, 128), 128)]
+        turned = pltpu.roll(tile, (j - spot) & 127, 1)
         total = jnp.where(lanes == j, turned, total)
     o_ref[...] = total
 
@@ -231,51 +241,81 @@
     )(scalars, gathered, couple_cond, couple_cap)
 
 
-def place_kernel(part, stride, group, nodes_ref, y_ref, extra_ref, *rest):
-    o_ref = rest[-1]
-    step = pl.program_id(0)
-    _, rows, width = y_ref.shape
-    per = extra_ref.shape[2]
+def spread_kernel(nodes_ref, extra_ref, o_ref):
+    t = pl.program_id(0)
+    rows = o_ref.shape[0]
+    per = extra_ref.shape[1]
     lanes = lax.broadcasted_iota(jnp.int32, (rows, 128), 1)
-    for g in range(group):
-        t = step * group + g
-        lo = g * stride + part * width
-        o_ref[:, g * width : (g + 1) * width] = y_ref[g]
-        extra = extra_ref[g]
-        for j in range(per):
-            local = nodes_ref[t * per + j] - t * stride - part * width
-            first = jnp.clip(local // 128, 0, width // 128 - 1) * 128
-            at = pl.ds(pl.multiple_of(g * width + first, 128), 128)
-            old = o_ref[:, at]
-            o_ref[:, at] = old + jnp.where(lanes + first == local, extra[:, j : j + 1], 0.0)
-
-
-def place(y, extra, nodes, part, held):
-    count, rows, width = y.shape
-    per = nodes.shape[0] // count
-    stride = width * PARTS
-    in_specs = [
-        pl.BlockSpec((1, rows, width), lambda t, n: (t, 0, 0)),
-        pl.BlockSpec((1, rows, per), lambda t, n: (t, 0, 0)),
-    ]
-    args = [y, extra]
-    aliases = {}
-    if held is not None:
-        in_specs.append(pl.BlockSpec(memory_space=pl.ANY))
-        args.append(held)
-        aliases = {3: 0}
-    return pl.pallas_call(
-        functools.partial(place_kernel, part, stride, 1),
+    o_ref[...] = jnp.zeros_like(o_ref)
+    extra = extra_ref[...]
+    for j in range(per):
+        spot = nodes_ref[t * per + j]
+        at = pl.ds(pl.multiple_of(spot & ~127, 128), 128)
+        o_ref[:, at] += jnp.where(lanes == (spot & 127), extra[:, j : j + 1], 0.0)
+
+
+def spread(extra, nodes, width):
+    count, rows, per = extra.shape
+    return pl.pallas_call(
+        spread_kernel,
         grid_spec=pltpu.PrefetchScalarGridSpec(
             num_scalar_prefetch=1,
             grid=(count,),
-            in_specs=in_specs,
-            out_specs=pl.BlockSpec((rows, width), lambda t, n: (0, t * PARTS + part)),
-        ),
-        out_shape=jax.ShapeDtypeStruct((rows, count * stride), F32),
-        input_output_aliases=aliases,
+            in_specs=[pl.BlockSpec((None, rows, per), lambda t, n: (t, 0, 0))],
+            out_specs=pl.BlockSpec((rows, width), lambda t, n: (0, t)),
+        ),
+        out_shape=jax.ShapeDtypeStruct((rows, count * width), F32),
+        name="spread",
+    )(nodes, extra)
+
+
+def place_kernel(part, stride, y_ref, held_ref, o_ref, y_buf, held_buf, sem_y, sem_held, sem_out):
+    count, _, width = y_ref.shape
+    at = [pl.ds(t * stride + part * width, width) for t in range(count)]
+    loads = [
+        (
+            pltpu.make_async_copy(y_ref.at[t], y_buf.at[t], sem_y.at[t]),
+            pltpu.make_async_copy(held_ref.at[:, at[t]], held_buf.at[t], sem_held.at[t]),
+        )
+        for t in range(count)
+    ]
+    stores = [
+        pltpu.make_async_copy(y_buf.at[t], o_ref.at[:, at[t]], sem_out.at[t])
+        for t in range(count)
+    ]
+    for first, second in loads:
+        first.start()
+        second.start()
+    for t in range(count):
+        loads[t][0].wait()
+        loads[t][1].wait()
+        y_buf[t] = y_buf[t] + held_buf[t]
+        stores[t].start()
+    for store in stores:
+        store.wait()
+
+
+def place(y, part, held):
+    count, rows, width = y.shape
+    return pl.pallas_call(
+        functools.partial(place_kernel, part, width * PARTS),
+        in_specs=[pl.BlockSpec(memory_space=pl.ANY)] * 2,
+        out_specs=pl.BlockSpec(memory_space=pl.ANY),
+        out_shape=jax.ShapeDtypeStruct(held.shape, F32),
+        scratch_shapes=[
+            pltpu.VMEM(y.shape, F32),
+            pltpu.VMEM(y.shape, F32),
+            pltpu.SemaphoreType.DMA((count,)),
+            pltpu.SemaphoreType.DMA((count,)),
+            pltpu.SemaphoreType.DMA((count,)),
+        ],
+        input_output_aliases={1: 0},
         name="place",
-    )(nodes, *args)
+    )(in_hbm(y), held)
+
+
+def in_hbm(x):
+    return pltpu.with_memory_space_constraint(x, pltpu.HBM)
 
 
 def shards(
@@ -295,7 +335,10 @@
     count = lax.axis_size("spec")
     basis_table, forward_table = fourier_tables(length)
     basis, forward = widened(basis_table), widened(forward_table)
+    stride = spectrum.shape[1] // count
     nodes = boundary_nodes[0]
+    slices = jnp.arange(nodes.shape[0], dtype=jnp.int32) // (nodes.shape[0] // count)
+    nodes = jnp.clip(nodes - slices * stride, 0, stride - 1)
     nodal_args = (conductance, capacitance, block_cond, block_cap, basis, forward)
 
     def swap(x):
@@ -303,11 +346,13 @@
 
     arrived = []
     for part in range(PARTS):
-        got = swap(pack(spectrum, part, count))
-        arrived.append(got.reshape(length, got.shape[2]))
-
-    own_boundary = pick(spectrum, nodes, count)
-    gathered = lax.all_gather(own_boundary, "dom", axis=0, tiled=False)
+        packed = pack(spectrum, part, count)
+        if part == 1:
+            own_boundary = pick(spectrum, nodes, count)
+            gathered = lax.all_gather(own_boundary, "dom", axis=0, tiled=False)
+            packed, gathered = lax.optimization_barrier((packed, gathered))
+        arrived.append(swap(packed))
+
     extra = couple(
         gathered,
         couple_src[0],
@@ -319,11 +364,15 @@
     )
     extra = extra.reshape(rows, count, nodes.shape[0] // count).transpose(1, 0, 2)
 
-    result = None
     for part in range(PARTS):
         current = nodal(part, arrived[part], *nodal_args)
-        back = swap(current.reshape(count, rows, current.shape[1]))
-        result = place(back, extra, nodes, part, result)
+        if part == 0:
+            current, extra = lax.optimization_barrier((current, extra))
+            result = spread(extra, nodes, stride)
+        if part == 1:
+            current, result = lax.optimization_barrier((current, result))
+        back = swap(current)
+        result = place(back, part, result)
     return result
 
 

time: 274 us -> 150 us (0.55)
  Pallas kernels: 184 us -> 52.7 us
  blocking collectives: 14.3 us -> 43.9 us
  waiting for transfers between devices: 39.3 us -> 26.3 us
  starting transfers between devices: 24.5 us -> 18.7 us
  local copies, waits for them, and re-layouts: 8.18 us -> 5.24 us
    pallas_call x2, Pallas kernels: 130 us -> 5.2 us  [pack(): pl.pallas_call(functools.partial(pack_kernel, part * width, stride), in_s...]
    all_to_all x0 -> x1, blocking collectives: none -> 29.5 us  [swap(): return lax.all_to_all(x, 'spec', split_axis=0, concat_axis=0, tiled=True)]
    all_to_all x4 -> x3, waiting for transfers between devices: 39.3 us -> 26.3 us  [swap(): return lax.all_to_all(x, 'spec', split_axis=0, concat_axis=0, tiled=True)]
    all_to_all x4 -> x3, starting transfers between devices: 24.5 us -> 18.7 us  [swap(): return lax.all_to_all(x, 'spec', split_axis=0, concat_axis=0, tiled=True)]
    pallas_call x2 -> x3, Pallas kernels: 22.2 us -> 17.6 us  [the longest x1 9.97 us: spread(): pl.pallas_call(spread_kernel, grid_spec=pltpu.PrefetchScalarGridSpec(num_...]
    unnamed x14 -> x18, local copies, waits for them, and re-layouts: 5.61 us -> 2.69 us
  transfers between devices with their start and end apart: 4 -> 3, of which waited for: 2 -> 3; matrix products, arithmetic and copies ran while one was open for 1% -> 3% of each run, Pallas kernels for 40% -> 29%
where the time goes in v1:
time: 150 us; the launch traced here: 149 us
  Pallas kernels  52.7 us (35%)
  blocking collectives  43.9 us (29%)
  waiting for transfers between devices  26.3 us (18%)
  starting transfers between devices  18.7 us (12%)
  local copies, waits for them, and re-layouts  5.24 us (3%)
    all_to_all x1, blocking collectives, swap(): return lax.all_to_all(x, 'spec', split_axis=0, concat_axis=0, tiled=True)  29.5 us
    all_to_all x3, waiting for transfers between devices, swap(): return lax.all_to_all(x, 'spec', split_axis=0, concat_axis=0, tiled=True)  26.3 us
    all_to_all x3, starting transfers between devices, swap(): return lax.all_to_all(x, 'spec', split_axis=0, concat_axis=0, tiled=True)  18.7 us
    all_gather x1, blocking collectives, shards(): gathered = lax.all_gather(own_boundary, 'dom', axis=0, tiled=False)  14.3 us
    pallas_call x2, Pallas kernels, nodal(): pl.pallas_call(functools.partial(nodal_kernel, length, block), grid=(step...  13.3 us
    pallas_call x1, Pallas kernels, pick(): pl.pallas_call(functools.partial(pick_kernel, per), grid_spec=pltpu.Prefe...  10.7 us
    pallas_call x1, Pallas kernels, spread(): pl.pallas_call(spread_kernel, grid_spec=pltpu.PrefetchScalarGridSpec(num_...  9.97 us
    pallas_call x2, Pallas kernels, place(): pl.pallas_call(functools.partial(place_kernel, part, width * PARTS), in_s...  7.61 us
  transfers between devices with their start and end apart: 3, of which 3 were waited for; matrix products, arithmetic and copies ran while one was open for 3% of the time, Pallas kernels for 29%

profile of v1, /device:TPU:0, one launch (start us, length us, event | category | flops | bytes accessed | tf_op | source)
XLA Modules:
  0.0 148.8 jit_solution(6933744294776754990)
XLA Ops:
  0.0 2.6 %pack.3 = f32[16,16,2048]{2,1,0:T(8,128)} custom-call(f32[16,65536]{1,0:T(8,128)} %x_ref.5), custom_call_target="tpu_custom_call" | custom-call | tf_op jit(solution)/shard_map/pack/pallas_call | solution.py:151
  2.6 8.0 %all-to-all-start.1 = ((f32[16,16,2048]{2,1,0:T(8,128)}), f32[16,16,2048]{2,1,0:T(8,128)S(1)}, u32[]{:S(2)}, u32[]{:S(2)}) async-start(f32[16,16,2048]{2,1,0:T(8,128)} %pack.3), calls=%async_computation.1 | async-start | bytes 4194304 | tf_op jit(solution)/shard_map/all_to_all | solution.py:345
  10.6 0.0 copy-start.7
  10.6 2.6 %pack.2 = f32[16,16,2048]{2,1,0:T(8,128)} custom-call(f32[16,65536]{1,0:T(8,128)} %x_ref.5), custom_call_target="tpu_custom_call" | custom-call | tf_op jit(solution)/shard_map/pack/pallas_call | solution.py:151
  13.2 0.0 copy-done.7
  13.2 0.6 fusion.2.nodes_ref
  13.8 10.7 %pick.1 = f32[16,16,128]{2,1,0:T(8,128)} custom-call(s32[256]{0:T(256)} %fusion.2.nodes_ref, f32[16,65536]{1,0:T(8,128)} %x_ref.5), custom_call_target="tpu_custom_call" | custom-call | tf_op jit(solution)/shard_map/pick/pallas_call | solution.py:180
  24.5 0.9 slice_bitcast_fusion
  25.5 0.1 all_gather_reshape.3
  25.6 14.3 %all_gather.3.x_ref = f32[8,16,256]{2,1,0:T(8,128)} all-gather(f32[1,16,256]{2,1,0:T(8,128)S(1)} %all_gather_reshape.3), channel_id=1, replica_groups=mesh['dom'=8,'spec'=16] {'dom'}, dimensions={0}, use_global_device_ids=true | all-gather | bytes 147456 | tf_op jit(solution)/shard_map/all_gather | solution.py:352
  39.9 0.0 copy-start.8
  39.9 1.1 all-to-all-done.1.s_ref
  41.0 0.0 copy-start.6
  41.0 6.3 %all-to-all-start = ((f32[16,16,2048]{2,1,0:T(8,128)}), f32[16,16,2048]{2,1,0:T(8,128)}, u32[]{:S(2)}, u32[]{:S(2)}) async-start(f32[16,16,2048]{2,1,0:T(8,128)} %pack.2), calls=%async_computation | async-start | bytes 4194304 | tf_op jit(solution)/shard_map/all_to_all | solution.py:345
  47.3 0.0 copy-done.6
  48.0 0.0 copy-done.8
  48.0 0.6 pad_add_fusion.scalars_ref
  48.6 0.0 copy-start
  48.6 0.0 copy-start.4
  48.6 0.0 copy-start.5
  48.6 6.0 %couple.1 = f32[16,256]{1,0:T(8,128)} custom-call(s32[9]{0:T(128)} %pad_add_fusion.scalars_ref, f32[8,16,256]{2,1,0:T(8,128)} %all_gather.3.x_ref, f32[1,7,256,256]{3,2,1,0:T(8,128)} %cond_ref.5, f32[1,7,256,256]{3,2,1,0:T(8,128)} %cap_ref.5), custom_call_target="tpu_custom_call" | custom-call | tf_op jit(solution)/shard_map/couple/pallas_call | solution.py:227
  54.6 0.8 reshape.3
  55.4 0.7 copy.22
  56.1 0.0 copy-done
  56.1 0.0 copy-done.4
  56.1 0.0 copy-done.5
  56.1 6.6 %nodal.3 = f32[16,16,2048]{2,1,0:T(8,128)S(1)} custom-call(f32[16,16,2048]{2,1,0:T(8,128)} %copy-done.6, f32[256,4096]{1,0:T(8,128)} %g_ref.3, f32[256,4096]{1,0:T(8,128)} %c_ref.3, f32[32,128,128]{2,1,0:T(8,128)S(1)} %copy-done, f32[32,128,128]{2,1,0:T(8,128)} %cap_ref.4, bf16[256,768]{1,0:T(8,128)(2,1)S(1)} %copy-done.5, bf16[256,768]{1,0:T(8,128)(2,1)S(1)} %copy-done.4), custom_call_target="tpu_custom_call" | custom-call | flops 3221225472 | bytes 10485760 | tf_op jit(solution)/shard_map/nodal/pallas_call | solution.py:105
  62.7 0.0 copy-start.1
  62.7 1.3 copy-done.1
  64.1 14.4 %all-to-all-done.s_ref = f32[16,16,2048]{2,1,0:T(8,128)} async-done(((f32[16,16,2048]{2,1,0:T(8,128)}), f32[16,16,2048]{2,1,0:T(8,128)}, u32[]{:S(2)}, u32[]{:S(2)}) %all-to-all-start) | async-done | bytes 2097184 | tf_op jit(solution)/shard_map/all_to_all | solution.py:345
  78.5 4.4 %all-to-all-start.2 = ((f32[16,16,2048]{2,1,0:T(8,128)}), f32[16,16,2048]{2,1,0:T(8,128)}, u32[]{:S(2)}, u32[]{:S(2)}) async-start(f32[16,16,2048]{2,1,0:T(8,128)} %copy-done.1), calls=%async_computation.2 | async-start | bytes 4194304 | tf_op jit(solution)/shard_map/all_to_all | solution.py:345
  82.9 10.0 %spread.1.held_ref = f32[16,65536]{1,0:T(8,128)} custom-call(s32[256]{0:T(256)} %fusion.2.nodes_ref, f32[16,16,16]{2,1,0:T(8,128)} %bitcast.8), custom_call_target="tpu_custom_call" | custom-call | tf_op jit(solution)/shard_map/spread/pallas_call | solution.py:259
  92.9 6.6 %nodal.2 = f32[16,16,2048]{2,1,0:T(8,128)S(1)} custom-call(f32[16,16,2048]{2,1,0:T(8,128)} %all-to-all-done.s_ref, f32[256,4096]{1,0:T(8,128)} %g_ref.3, f32[256,4096]{1,0:T(8,128)} %c_ref.3, f32[32,128,128]{2,1,0:T(8,128)S(1)} %copy-done, f32[32,128,128]{2,1,0:T(8,128)} %cap_ref.4, bf16[256,768]{1,0:T(8,128)(2,1)S(1)} %copy-done.5, ...), custom_call_target="tpu_custom_call" | custom-call | flops 3221225472 | bytes 10485760 | tf_op jit(solution)/shard_map/nodal/pallas_call | solution.py:105
  99.6 0.0 copy-start.2
  99.6 1.3 copy-done.2
  100.9 10.7 %all-to-all-done.2.y_ref = f32[16,16,2048]{2,1,0:T(8,128)} async-done(((f32[16,16,2048]{2,1,0:T(8,128)}), f32[16,16,2048]{2,1,0:T(8,128)}, u32[]{:S(2)}, u32[]{:S(2)}) %all-to-all-start.2) | async-done | bytes 2097184 | tf_op jit(solution)/shard_map/all_to_all | solution.py:345
  111.6 0.0 copy-start.3
  111.6 3.9 %place.2.held_ref = f32[16,65536]{1,0:T(8,128)} custom-call(f32[16,16,2048]{2,1,0:T(8,128)} %all-to-all-done.2.y_ref, f32[16,65536]{1,0:T(8,128)} %spread.1.held_ref), custom_call_target="tpu_custom_call", output_to_operand_aliasing={{}: (1, {})} | custom-call | tf_op jit(solution)/shard_map/place/pallas_call | solution.py:300
  115.5 0.0 copy-done.3
  115.5 29.5 %all_to_all.20.y_ref = f32[16,16,2048]{2,1,0:T(8,128)} all-to-all(f32[16,16,2048]{2,1,0:T(8,128)S(1)} %copy-done.3), channel_id=1, replica_groups=mesh['dom'=8,'spec'=16] {'spec'}, dimensions={0} | all-to-all | bytes 4194304 | tf_op jit(solution)/shard_map/all_to_all | solution.py:345
  145.0 3.7 %place.3 = f32[16,65536]{1,0:T(8,128)} custom-call(f32[16,16,2048]{2,1,0:T(8,128)} %all_to_all.20.y_ref, f32[16,65536]{1,0:T(8,128)} %place.2.held_ref), custom_call_target="tpu_custom_call", output_to_operand_aliasing={{}: (1, {})} | custom-call | tf_op jit(solution)/shard_map/place/pallas_call | solution.py:300
  (1 shorter events, 0.0 us)
Async XLA Ops:
  2.6 38.4 %all-to-all-start.1 = ((f32[16,16,2048]{2,1,0:T(8,128)}), f32[16,16,2048]{2,1,0:T(8,128)S(1)}, u32[]{:S(2)}, u32[]{:S(2)}) async-start(f32[16,16,2048]{2,1,0:T(8,128)} %pack.3), calls=%async_computation.1 | async-start | bytes 4194304 | tf_op jit(solution)/shard_map/all_to_all | solution.py:345
  10.6 2.6 %copy-start.7 = (s32[1,256]{1,0:T(1,128)S(1)}, s32[1,256]{1,0:T(1,128)}, u32[]{:S(2)}) copy-start(s32[1,256]{1,0:T(1,128)} %param.17) | copy-start | bytes 3076
  39.9 8.1 %copy-start.8 = (s32[1,7]{1,0:T(1,128)S(1)}, s32[1,7]{1,0:T(1,128)}, u32[]{:S(2)}) copy-start(s32[1,7]{1,0:T(1,128)} %param.18) | copy-start | bytes 88
  41.0 6.3 %copy-start.6 = (f32[16,16,2048]{2,1,0:T(8,128)}, f32[16,16,2048]{2,1,0:T(8,128)S(1)}, u32[]{:S(2)}) copy-start(f32[16,16,2048]{2,1,0:T(8,128)S(1)} %all-to-all-done.1.s_ref) | copy-start | bytes 6291460
  41.0 37.5 %all-to-all-start = ((f32[16,16,2048]{2,1,0:T(8,128)}), f32[16,16,2048]{2,1,0:T(8,128)}, u32[]{:S(2)}, u32[]{:S(2)}) async-start(f32[16,16,2048]{2,1,0:T(8,128)} %pack.2), calls=%async_computation | async-start | bytes 4194304 | tf_op jit(solution)/shard_map/all_to_all | solution.py:345
  48.6 7.5 %copy-start = (f32[32,128,128]{2,1,0:T(8,128)S(1)}, f32[32,128,128]{2,1,0:T(8,128)}, u32[]{:S(2)}) copy-start(f32[32,128,128]{2,1,0:T(8,128)} %cond_ref.4) | copy-start | bytes 6291460
  48.6 7.5 %copy-start.4 = (bf16[256,768]{1,0:T(8,128)(2,1)S(1)}, bf16[256,768]{1,0:T(8,128)(2,1)}, u32[]{:S(2)}) copy-start(bf16[256,768]{1,0:T(8,128)(2,1)} %constant.33.clone.forward_ref) | copy-start | bytes 1179652
  48.6 7.5 %copy-start.5 = (bf16[256,768]{1,0:T(8,128)(2,1)S(1)}, bf16[256,768]{1,0:T(8,128)(2,1)}, u32[]{:S(2)}) copy-start(bf16[256,768]{1,0:T(8,128)(2,1)} %constant.32.clone.basis_ref) | copy-start | bytes 1179652
  62.7 1.3 copy-start.1
  78.5 33.1 %all-to-all-start.2 = ((f32[16,16,2048]{2,1,0:T(8,128)}), f32[16,16,2048]{2,1,0:T(8,128)}, u32[]{:S(2)}, u32[]{:S(2)}) async-start(f32[16,16,2048]{2,1,0:T(8,128)} %copy-done.1), calls=%async_computation.2 | async-start | bytes 4194304 | tf_op jit(solution)/shard_map/all_to_all | solution.py:345
  99.6 1.3 copy-start.2
  111.6 3.9 %copy-start.3 = (f32[16,16,2048]{2,1,0:T(8,128)S(1)}, f32[16,16,2048]{2,1,0:T(8,128)}, u32[]{:S(2)}) copy-start(f32[16,16,2048]{2,1,0:T(8,128)} %copy-done.2) | copy-start | bytes 6291460

commit v2 on v1

--- a/solution.py
+++ b/solution.py
@@ -13,6 +13,8 @@
 BF16 = jnp.bfloat16
 PARTS = 2
 TILE = 512
+GROUP = 4
+EARLY = 4
 
 
 def fourier_tables(length):
@@ -162,28 +164,31 @@
     )(x)
 
 
-def pick_kernel(per, nodes_ref, x_ref, o_ref):
-    t = pl.program_id(0)
+def pick_kernel(per, stride, nodes_ref, x_ref, o_ref):
+    group = o_ref.shape[0]
     lanes = lax.broadcasted_iota(jnp.int32, (x_ref.shape[0], 128), 1)
-    total = jnp.zeros((x_ref.shape[0], 128), F32)
-    for j in range(per):
-        spot = nodes_ref[t * per + j]
-        tile = x_ref[:, pl.ds(pl.multiple_of(spot & ~127, 128), 128)]
-        turned = pltpu.roll(tile, (j - spot) & 127, 1)
-        total = jnp.where(lanes == j, turned, total)
-    o_ref[...] = total
+    for g in range(group):
+        t = pl.program_id(0) * group + g
+        total = jnp.zeros((x_ref.shape[0], 128), F32)
+        for j in range(per):
+            spot = nodes_ref[t * per + j] + g * stride
+            tile = x_ref[:, pl.ds(pl.multiple_of(spot & ~127, 128), 128)]
+            turned = pltpu.roll(tile, (j - spot) & 127, 1)
+            total = jnp.where(lanes == j, turned, total)
+        o_ref[g] = total
 
 
 def pick(x, nodes, count):
     rows, columns = x.shape
     per = nodes.shape[0] // count
+    stride = columns // count
     picked = pl.pallas_call(
-        functools.partial(pick_kernel, per),
+        functools.partial(pick_kernel, per, stride),
         grid_spec=pltpu.PrefetchScalarGridSpec(
             num_scalar_prefetch=1,
-            grid=(count,),
-            in_specs=[pl.BlockSpec((rows, columns // count), lambda t, n: (0, t))],
-            out_specs=pl.BlockSpec((None, rows, 128), lambda t, n: (t, 0, 0)),
+            grid=(count // GROUP,),
+            in_specs=[pl.BlockSpec((rows, GROUP * stride), lambda t, n: (0, t))],
+            out_specs=pl.BlockSpec((GROUP, rows, 128), lambda t, n: (t, 0, 0)),
         ),
         out_shape=jax.ShapeDtypeStruct((count, rows, 128), F32),
         name="pick",
@@ -241,77 +246,83 @@
     )(scalars, gathered, couple_cond, couple_cap)
 
 
-def spread_kernel(nodes_ref, extra_ref, o_ref):
-    t = pl.program_id(0)
-    rows = o_ref.shape[0]
-    per = extra_ref.shape[1]
+def spread_kernel(stride, nodes_ref, extra_ref, o_ref):
+    group, rows, per = extra_ref.shape
     lanes = lax.broadcasted_iota(jnp.int32, (rows, 128), 1)
     o_ref[...] = jnp.zeros_like(o_ref)
-    extra = extra_ref[...]
-    for j in range(per):
-        spot = nodes_ref[t * per + j]
-        at = pl.ds(pl.multiple_of(spot & ~127, 128), 128)
-        o_ref[:, at] += jnp.where(lanes == (spot & 127), extra[:, j : j + 1], 0.0)
-
-
-def spread(extra, nodes, width):
+    for g in range(group):
+        t = pl.program_id(0) * group + g
+        extra = extra_ref[g]
+        for j in range(per):
+            spot = nodes_ref[t * per + j] + g * stride
+            at = pl.ds(pl.multiple_of(spot & ~127, 128), 128)
+            o_ref[:, at] += jnp.where(lanes == (spot & 127), extra[:, j : j + 1], 0.0)
+
+
+def spread(extra, nodes, stride):
     count, rows, per = extra.shape
     return pl.pallas_call(
-        spread_kernel,
+        functools.partial(spread_kernel, stride),
         grid_spec=pltpu.PrefetchScalarGridSpec(
             num_scalar_prefetch=1,
-            grid=(count,),
-            in_specs=[pl.BlockSpec((None, rows, per), lambda t, n: (t, 0, 0))],
-            out_specs=pl.BlockSpec((rows, width), lambda t, n: (0, t)),
+            grid=(count // GROUP,),
+            in_specs=[pl.BlockSpec((GROUP, rows, per), lambda t, n: (t, 0, 0))],
+            out_specs=pl.BlockSpec((rows, GROUP * stride), lambda t, n: (0, t)),
         ),
-        out_shape=jax.ShapeDtypeStruct((rows, count * width), F32),
+        out_shape=jax.ShapeDtypeStruct((rows, count * stride), F32),
         name="spread",
     )(nodes, extra)
 
 
-def place_kernel(part, stride, y_ref, held_ref, o_ref, y_buf, held_buf, sem_y, sem_held, sem_out):
-    count, _, width = y_ref.shape
-    at = [pl.ds(t * stride + part * width, width) for t in range(count)]
+def place_kernel(*refs):
+    y_refs, held_ref, o_ref = refs[:PARTS], refs[PARTS], refs[PARTS + 1]
+    y_buf, held_buf, sem_y, sem_held, sem_out = refs[PARTS + 2 :]
+    count, _, width = y_refs[0].shape
+    at = [pl.ds(t * width * PARTS, width * PARTS) for t in range(count)]
     loads = [
-        (
-            pltpu.make_async_copy(y_ref.at[t], y_buf.at[t], sem_y.at[t]),
-            pltpu.make_async_copy(held_ref.at[:, at[t]], held_buf.at[t], sem_held.at[t]),
-        )
+        [pltpu.make_async_copy(held_ref.at[:, at[t]], held_buf.at[t], sem_held.at[t])]
+        + [
+            pltpu.make_async_copy(
+                y_refs[p].at[t], y_buf.at[t, :, pl.ds(p * width, width)], sem_y.at[p, t]
+            )
+            for p in range(PARTS)
+        ]
         for t in range(count)
     ]
     stores = [
         pltpu.make_async_copy(y_buf.at[t], o_ref.at[:, at[t]], sem_out.at[t])
         for t in range(count)
     ]
-    for first, second in loads:
-        first.start()
-        second.start()
+    for group in loads:
+        for load in group:
+            load.start()
     for t in range(count):
-        loads[t][0].wait()
-        loads[t][1].wait()
+        for load in loads[t]:
+            load.wait()
         y_buf[t] = y_buf[t] + held_buf[t]
         stores[t].start()
     for store in stores:
         store.wait()
 
 
-def place(y, part, held):
-    count, rows, width = y.shape
+def place(ys, held):
+    count, rows, width = ys[0].shape
+    whole = (count, rows, width * PARTS)
     return pl.pallas_call(
-        functools.partial(place_kernel, part, width * PARTS),
-        in_specs=[pl.BlockSpec(memory_space=pl.ANY)] * 2,
+        place_kernel,
+        in_specs=[pl.BlockSpec(memory_space=pl.ANY)] * (PARTS + 1),
         out_specs=pl.BlockSpec(memory_space=pl.ANY),
         out_shape=jax.ShapeDtypeStruct(held.shape, F32),
         scratch_shapes=[
-            pltpu.VMEM(y.shape, F32),
-            pltpu.VMEM(y.shape, F32),
-            pltpu.SemaphoreType.DMA((count,)),
+            pltpu.VMEM(whole, F32),
+            pltpu.VMEM(whole, F32),
+            pltpu.SemaphoreType.DMA((PARTS, count)),
             pltpu.SemaphoreType.DMA((count,)),
             pltpu.SemaphoreType.DMA((count,)),
         ],
-        input_output_aliases={1: 0},
+        compiler_params=pltpu.CompilerParams(vmem_limit_bytes=48 << 20),
         name="place",
-    )(in_hbm(y), held)
+    )(*[in_hbm(y) for y in ys], held)
 
 
 def in_hbm(x):
@@ -333,6 +344,7 @@
     length = conductance.shape[0]
     rows = spectrum.shape[0]
     count = lax.axis_size("spec")
+    doms = lax.axis_size("dom")
     basis_table, forward_table = fourier_tables(length)
     basis, forward = widened(basis_table), widened(forward_table)
     stride = spectrum.shape[1] // count
@@ -349,13 +361,20 @@
         packed = pack(spectrum, part, count)
         if part == 1:
             own_boundary = pick(spectrum, nodes, count)
-            gathered = lax.all_gather(own_boundary, "dom", axis=0, tiled=False)
-            packed, gathered = lax.optimization_barrier((packed, gathered))
+            moved = [
+                lax.ppermute(own_boundary, "dom", [(d, (d + k) % doms) for d in range(doms)])
+                for k in range(1, doms)
+            ]
+            packed, moved[:EARLY] = lax.optimization_barrier((packed, moved[:EARLY]))
         arrived.append(swap(packed))
 
+    current = nodal(0, arrived[0], *nodal_args)
+    current, moved = lax.optimization_barrier((current, moved))
+    first = swap(current)
+
     extra = couple(
-        gathered,
-        couple_src[0],
+        jnp.stack(moved),
+        (lax.axis_index("dom") - couple_src[0]) % doms - 1,
         couple_count,
         lax.axis_index("spec") * rows,
         length,
@@ -364,16 +383,10 @@
     )
     extra = extra.reshape(rows, count, nodes.shape[0] // count).transpose(1, 0, 2)
 
-    for part in range(PARTS):
-        current = nodal(part, arrived[part], *nodal_args)
-        if part == 0:
-            current, extra = lax.optimization_barrier((current, extra))
-            result = spread(extra, nodes, stride)
-        if part == 1:
-            current, result = lax.optimization_barrier((current, result))
-        back = swap(current)
-        result = place(back, part, result)
-    return result
+    held = spread(extra, nodes, stride)
+    current = nodal(1, arrived[1], *nodal_args)
+    current, held = lax.optimization_barrier((current, held))
+    return place([first, swap(current)], held)
 
 
 def solution(mesh):

time: 150 us -> 141 us (0.940)
  Pallas kernels: 52.7 us -> 38.6 us
  blocking collectives: 43.9 us -> 30.7 us
  waiting for transfers between devices: 26.3 us -> 37.6 us
  starting transfers between devices: 18.7 us -> 25.4 us
    all_gather x1 -> x0, blocking collectives: 14.3 us -> none  [shards(): gathered = lax.all_gather(own_boundary, 'dom', axis=0, tiled=False)]
    pallas_call x4 -> x3, Pallas kernels: 28.3 us -> 14.3 us  [the longest x1 4.98 us: spread(): pl.pallas_call(functools.partial(spread_kernel, stride), grid_spec=pltpu....]
    all_to_all x3, waiting for transfers between devices: 26.3 us -> 37 us  [swap(): return lax.all_to_all(x, 'spec', split_axis=0, concat_axis=0, tiled=True)]
    ppermute x0 -> x7, starting transfers between devices: none -> 8.52 us  [shards(): lax.ppermute(own_boundary, 'dom', [(d, (d + k) % doms) for d in range(dom...]
    all_to_all x3, starting transfers between devices: 18.7 us -> 16.9 us  [swap(): return lax.all_to_all(x, 'spec', split_axis=0, concat_axis=0, tiled=True)]
    unnamed x18 -> x24, local copies, waits for them, and re-layouts: 2.69 us -> 3.33 us
  transfers between devices with their start and end apart: 3 -> 10, of which waited for: 3 -> 6; matrix products, arithmetic and copies ran while one was open for 3% -> 3% of each run, Pallas kernels for 29% -> 22%
where the time goes in v2:
time: 141 us; the launch traced here: 140 us
  Pallas kernels  38.6 us (27%)
  waiting for transfers between devices  37.6 us (27%)
  blocking collectives  30.7 us (22%)
  starting transfers between devices  25.4 us (18%)
  local copies, waits for them, and re-layouts  5.9 us (4%)
    all_to_all x3, waiting for transfers between devices, swap(): return lax.all_to_all(x, 'spec', split_axis=0, concat_axis=0, tiled=True)  37 us
    all_to_all x1, blocking collectives, swap(): return lax.all_to_all(x, 'spec', split_axis=0, concat_axis=0, tiled=True)  30.7 us
    all_to_all x3, starting transfers between devices, swap(): return lax.all_to_all(x, 'spec', split_axis=0, concat_axis=0, tiled=True)  16.9 us
    pallas_call x2, Pallas kernels, nodal(): pl.pallas_call(functools.partial(nodal_kernel, length, block), grid=(step...  13.3 us
    ppermute x7, starting transfers between devices, shards(): lax.ppermute(own_boundary, 'dom', [(d, (d + k) % doms) for d in range(dom...  8.52 us
    pallas_call x1, Pallas kernels, couple(): pl.pallas_call(functools.partial(couple_kernel, length), grid_spec=pltpu....  5.79 us
    pallas_call x2, Pallas kernels, pack(): pl.pallas_call(functools.partial(pack_kernel, part * width, stride), in_s...  5.22 us
    pallas_call x1, Pallas kernels, spread(): pl.pallas_call(functools.partial(spread_kernel, stride), grid_spec=pltpu....  4.98 us
  transfers between devices with their start and end apart: 10, of which 6 were waited for; matrix products, arithmetic and copies ran while one was open for 3% of the time, Pallas kernels for 22%

profile of v2, /device:TPU:0, one launch (start us, length us, event | category | flops | bytes accessed | tf_op | source)
XLA Modules:
  0.0 140.4 jit_solution(2592559059778468117)
XLA Ops:
  0.0 2.6 %pack.2 = f32[16,16,2048]{2,1,0:T(8,128)} custom-call(f32[16,65536]{1,0:T(8,128)} %x_ref.5), custom_call_target="tpu_custom_call" | custom-call | tf_op jit(solution)/shard_map/pack/pallas_call | solution.py:153
  2.6 0.0 copy-start.7
  2.6 8.0 %all-to-all-start = ((f32[16,16,2048]{2,1,0:T(8,128)}), f32[16,16,2048]{2,1,0:T(8,128)}, u32[]{:S(2)}, u32[]{:S(2)}) async-start(f32[16,16,2048]{2,1,0:T(8,128)} %pack.2), calls=%async_computation | async-start | bytes 4194304 | tf_op jit(solution)/shard_map/all_to_all | solution.py:357
  10.6 0.0 copy-done.7
  10.6 0.6 fusion.2.nodes_ref
  11.2 4.9 %pick.1 = f32[16,16,128]{2,1,0:T(8,128)} custom-call(s32[256]{0:T(256)} %fusion.2.nodes_ref, f32[16,65536]{1,0:T(8,128)} %x_ref.5), custom_call_target="tpu_custom_call" | custom-call | tf_op jit(solution)/shard_map/pick/pallas_call | solution.py:185
  16.1 0.9 slice_bitcast_fusion
  17.1 0.1 reshape.8
  17.2 3.3 %collective-permute-start.3 = (f32[16,256]{1,0:T(8,128)S(1)}, f32[16,256]{1,0:T(8,128)S(1)}, u32[]{:S(2)}, u32[]{:S(2)}) collective-permute-start(f32[16,256]{1,0:T(8,128)S(1)} %reshape.8), channel_id=1, source_target_pairs={{0,64},{16,80},{32,96},{48,112},{64,0},{80,16},{96,32},{112,48},{1... | collective-permute-start | bytes 49160 | tf_op jit(solution)/shard_map/ppermute | solution.py:365
  20.4 0.0 collective-permute-start.2
  20.4 0.7 collective-permute-start.1
  21.1 1.1 collective-permute-start
  22.2 2.7 %pack.3 = f32[16,16,2048]{2,1,0:T(8,128)} custom-call(f32[16,65536]{1,0:T(8,128)} %x_ref.5), custom_call_target="tpu_custom_call" | custom-call | tf_op jit(solution)/shard_map/pack/pallas_call | solution.py:153
  24.9 0.0 copy-start.8
  24.9 0.0 copy-start.1
  24.9 0.0 copy-start.4
  24.9 0.0 copy-start.5
  24.9 0.0 collective-permute-done.3
  24.9 0.2 collective-permute-done.2
  25.1 0.4 collective-permute-done.1
  25.5 0.1 collective-permute-done
  25.6 15.5 %all-to-all-done.s_ref = f32[16,16,2048]{2,1,0:T(8,128)} async-done(((f32[16,16,2048]{2,1,0:T(8,128)}), f32[16,16,2048]{2,1,0:T(8,128)}, u32[]{:S(2)}, u32[]{:S(2)}) %all-to-all-start) | async-done | bytes 2097184 | tf_op jit(solution)/shard_map/all_to_all | solution.py:357
  41.1 4.4 %all-to-all-start.2 = ((f32[16,16,2048]{2,1,0:T(8,128)}), f32[16,16,2048]{2,1,0:T(8,128)}, u32[]{:S(2)}, u32[]{:S(2)}) async-start(f32[16,16,2048]{2,1,0:T(8,128)} %pack.3), calls=%async_computation.2 | async-start | bytes 4194304 | tf_op jit(solution)/shard_map/all_to_all | solution.py:357
  45.5 0.0 collective-permute-start.6
  45.5 3.1 %collective-permute-start.5 = (f32[16,256]{1,0:T(8,128)S(1)}, f32[16,256]{1,0:T(8,128)S(1)}, u32[]{:S(2)}, u32[]{:S(2)}) collective-permute-start(f32[16,256]{1,0:T(8,128)S(1)} %reshape.8), channel_id=1, source_target_pairs={{0,96},{16,112},{32,0},{48,16},{64,32},{80,48},{96,64},{112,80},{1... | collective-permute-start | bytes 49160 | tf_op jit(solution)/shard_map/ppermute | solution.py:365
  48.6 0.4 collective-permute-start.4
  49.7 0.0 copy-done.8
  49.7 0.0 copy-done.1
  49.7 0.0 copy-done.4
  49.7 0.0 copy-done.5
  49.7 6.6 %nodal.2 = f32[16,16,2048]{2,1,0:T(8,128)S(1)} custom-call(f32[16,16,2048]{2,1,0:T(8,128)} %all-to-all-done.s_ref, f32[256,4096]{1,0:T(8,128)} %g_ref.3, f32[256,4096]{1,0:T(8,128)} %c_ref.3, f32[32,128,128]{2,1,0:T(8,128)S(1)} %copy-done.1, f32[32,128,128]{2,1,0:T(8,128)} %cap_ref.4, bf16[256,768]{1,0:T(8,128)(2,1)S(1)} %copy-done.5, ...), custom_call_target="tpu_custom_call" | custom-call | flops 3221225472 | bytes 10485760 | tf_op jit(solution)/shard_map/nodal/pallas_call | solution.py:107
  56.4 0.0 copy-start.2
  56.4 1.3 copy-done.2
  57.7 0.0 collective-permute-done.6
  57.7 0.0 collective-permute-done.5
  57.7 0.0 collective-permute-done.4
  57.7 15.4 %all-to-all-done.2.s_ref = f32[16,16,2048]{2,1,0:T(8,128)} async-done(((f32[16,16,2048]{2,1,0:T(8,128)}), f32[16,16,2048]{2,1,0:T(8,128)}, u32[]{:S(2)}, u32[]{:S(2)}) %all-to-all-start.2) | async-done | bytes 2097184 | tf_op jit(solution)/shard_map/all_to_all | solution.py:357
  73.2 4.4 %all-to-all-start.1 = ((f32[16,16,2048]{2,1,0:T(8,128)}), f32[16,16,2048]{2,1,0:T(8,128)}, u32[]{:S(2)}, u32[]{:S(2)}) async-start(f32[16,16,2048]{2,1,0:T(8,128)} %copy-done.2), calls=%async_computation.1 | async-start | bytes 4194304 | tf_op jit(solution)/shard_map/all_to_all | solution.py:357
  77.6 0.7 pad_add_fusion.scalars_ref
  78.3 0.0 copy-start.6
  78.3 0.6 copy-done.6
  79.0 5.8 %couple.1 = f32[16,256]{1,0:T(8,128)} custom-call(s32[9]{0:T(128)} %pad_add_fusion.scalars_ref, f32[7,16,256]{2,1,0:T(8,128)} %copy-done.6, f32[1,7,256,256]{3,2,1,0:T(8,128)} %cond_ref.5, f32[1,7,256,256]{3,2,1,0:T(8,128)} %cap_ref.5), custom_call_target="tpu_custom_call" | custom-call | tf_op jit(solution)/shard_map/couple/pallas_call | solution.py:232
  84.8 0.8 reshape.9
  85.6 0.7 copy.17
  86.3 5.0 %spread.1.refs_2_ = f32[16,65536]{1,0:T(8,128)} custom-call(s32[256]{0:T(256)} %fusion.2.nodes_ref, f32[16,16,16]{2,1,0:T(8,128)} %bitcast.23), custom_call_target="tpu_custom_call" | custom-call | tf_op jit(solution)/shard_map/spread/pallas_call | solution.py:264
  91.2 6.6 %nodal.3 = f32[16,16,2048]{2,1,0:T(8,128)S(1)} custom-call(f32[16,16,2048]{2,1,0:T(8,128)} %all-to-all-done.2.s_ref, f32[256,4096]{1,0:T(8,128)} %g_ref.3, f32[256,4096]{1,0:T(8,128)} %c_ref.3, f32[32,128,128]{2,1,0:T(8,128)S(1)} %copy-done.1, f32[32,128,128]{2,1,0:T(8,128)} %cap_ref.4, bf16[256,768]{1,0:T(8,128)(2,1)S(1)} %copy-done.5, ...), custom_call_target="tpu_custom_call" | custom-call | flops 3221225472 | bytes 10485760 | tf_op jit(solution)/shard_map/nodal/pallas_call | solution.py:107
  97.9 0.0 copy-start.3
  97.9 1.3 copy-done.3
  99.2 6.1 %all-to-all-done.1.refs_0_ = f32[16,16,2048]{2,1,0:T(8,128)} async-done(((f32[16,16,2048]{2,1,0:T(8,128)}), f32[16,16,2048]{2,1,0:T(8,128)}, u32[]{:S(2)}, u32[]{:S(2)}) %all-to-all-start.1) | async-done | bytes 2097184 | tf_op jit(solution)/shard_map/all_to_all | solution.py:357
  105.2 0.0 copy-start
  105.2 30.7 %all_to_all.20.refs_1_ = f32[16,16,2048]{2,1,0:T(8,128)} all-to-all(f32[16,16,2048]{2,1,0:T(8,128)} %copy-done.3), channel_id=1, replica_groups=mesh['dom'=8,'spec'=16] {'spec'}, dimensions={0} | all-to-all | bytes 4194304 | tf_op jit(solution)/shard_map/all_to_all | solution.py:357
  135.9 0.0 copy-done
  135.9 4.5 %place.1 = f32[16,65536]{1,0:T(8,128)} custom-call(f32[16,16,2048]{2,1,0:T(8,128)} %all-to-all-done.1.refs_0_, f32[16,16,2048]{2,1,0:T(8,128)} %all_to_all.20.refs_1_, f32[16,65536]{1,0:T(8,128)S(1)} %copy-done), custom_call_target="tpu_custom_call" | custom-call | tf_op jit(solution)/shard_map/place/pallas_call | solution.py:311
  (9 shorter events, 0.1 us)
Async XLA Ops:
  2.6 8.0 %copy-start.7 = (s32[1,256]{1,0:T(1,128)S(1)}, s32[1,256]{1,0:T(1,128)}, u32[]{:S(2)}) copy-start(s32[1,256]{1,0:T(1,128)} %param.17) | copy-start | bytes 3076
  2.6 38.5 %all-to-all-start = ((f32[16,16,2048]{2,1,0:T(8,128)}), f32[16,16,2048]{2,1,0:T(8,128)}, u32[]{:S(2)}, u32[]{:S(2)}) async-start(f32[16,16,2048]{2,1,0:T(8,128)} %pack.2), calls=%async_computation | async-start | bytes 4194304 | tf_op jit(solution)/shard_map/all_to_all | solution.py:357
  17.2 7.7 %collective-permute-start.3 = (f32[16,256]{1,0:T(8,128)S(1)}, f32[16,256]{1,0:T(8,128)S(1)}, u32[]{:S(2)}, u32[]{:S(2)}) collective-permute-start(f32[16,256]{1,0:T(8,128)S(1)} %reshape.8), channel_id=1, source_target_pairs={{0,64},{16,80},{32,96},{48,112},{64,0},{80,16},{96,32},{112,48},{1... | collective-permute-start | bytes 49160 | tf_op jit(solution)/shard_map/ppermute | solution.py:365
  20.4 4.7 %collective-permute-start.2 = (f32[16,256]{1,0:T(8,128)S(1)}, f32[16,256]{1,0:T(8,128)S(1)}, u32[]{:S(2)}, u32[]{:S(2)}) collective-permute-start(f32[16,256]{1,0:T(8,128)S(1)} %reshape.8), channel_id=1, source_target_pairs={{0,48},{16,64},{32,80},{48,96},{64,112},{80,0},{96,16},{112,32},{1... | collective-permute-start | bytes 49160 | tf_op jit(solution)/shard_map/ppermute | solution.py:365
  20.4 5.0 %collective-permute-start.1 = (f32[16,256]{1,0:T(8,128)S(1)}, f32[16,256]{1,0:T(8,128)S(1)}, u32[]{:S(2)}, u32[]{:S(2)}) collective-permute-start(f32[16,256]{1,0:T(8,128)S(1)} %reshape.8), channel_id=1, source_target_pairs={{0,32},{16,48},{32,64},{48,80},{64,96},{80,112},{96,0},{112,16},{1... | collective-permute-start | bytes 49160 | tf_op jit(solution)/shard_map/ppermute | solution.py:365
  21.1 4.4 %collective-permute-start = (f32[16,256]{1,0:T(8,128)S(1)}, f32[16,256]{1,0:T(8,128)S(1)}, u32[]{:S(2)}, u32[]{:S(2)}) collective-permute-start(f32[16,256]{1,0:T(8,128)S(1)} %reshape.8), channel_id=1, source_target_pairs={{0,16},{16,32},{32,48},{48,64},{64,80},{80,96},{96,112},{112,0},{1... | collective-permute-start | bytes 49160 | tf_op jit(solution)/shard_map/ppermute | solution.py:365
  24.9 24.8 %copy-start.8 = (s32[1,7]{1,0:T(1,128)S(1)}, s32[1,7]{1,0:T(1,128)}, u32[]{:S(2)}) copy-start(s32[1,7]{1,0:T(1,128)} %param.18) | copy-start | bytes 88
  24.9 24.8 %copy-start.1 = (f32[32,128,128]{2,1,0:T(8,128)S(1)}, f32[32,128,128]{2,1,0:T(8,128)}, u32[]{:S(2)}) copy-start(f32[32,128,128]{2,1,0:T(8,128)} %cond_ref.4) | copy-start | bytes 6291460
  24.9 24.8 %copy-start.4 = (bf16[256,768]{1,0:T(8,128)(2,1)S(1)}, bf16[256,768]{1,0:T(8,128)(2,1)}, u32[]{:S(2)}) copy-start(bf16[256,768]{1,0:T(8,128)(2,1)} %constant.54.clone.forward_ref) | copy-start | bytes 1179652
  24.9 24.8 %copy-start.5 = (bf16[256,768]{1,0:T(8,128)(2,1)S(1)}, bf16[256,768]{1,0:T(8,128)(2,1)}, u32[]{:S(2)}) copy-start(bf16[256,768]{1,0:T(8,128)(2,1)} %constant.53.clone.basis_ref) | copy-start | bytes 1179652
  41.1 32.1 %all-to-all-start.2 = ((f32[16,16,2048]{2,1,0:T(8,128)}), f32[16,16,2048]{2,1,0:T(8,128)}, u32[]{:S(2)}, u32[]{:S(2)}) async-start(f32[16,16,2048]{2,1,0:T(8,128)} %pack.3), calls=%async_computation.2 | async-start | bytes 4194304 | tf_op jit(solution)/shard_map/all_to_all | solution.py:357
  45.5 12.2 %collective-permute-start.6 = (f32[16,256]{1,0:T(8,128)S(1)}, f32[16,256]{1,0:T(8,128)S(1)}, u32[]{:S(2)}, u32[]{:S(2)}) collective-permute-start(f32[16,256]{1,0:T(8,128)S(1)} %reshape.8), channel_id=1, source_target_pairs={{0,112},{16,0},{32,16},{48,32},{64,48},{80,64},{96,80},{112,96},{1... | collective-permute-start | bytes 49160 | tf_op jit(solution)/shard_map/ppermute | solution.py:365
  45.5 12.2 %collective-permute-start.5 = (f32[16,256]{1,0:T(8,128)S(1)}, f32[16,256]{1,0:T(8,128)S(1)}, u32[]{:S(2)}, u32[]{:S(2)}) collective-permute-start(f32[16,256]{1,0:T(8,128)S(1)} %reshape.8), channel_id=1, source_target_pairs={{0,96},{16,112},{32,0},{48,16},{64,32},{80,48},{96,64},{112,80},{1... | collective-permute-start | bytes 49160 | tf_op jit(solution)/shard_map/ppermute | solution.py:365
  48.6 9.1 %collective-permute-start.4 = (f32[16,256]{1,0:T(8,128)S(1)}, f32[16,256]{1,0:T(8,128)S(1)}, u32[]{:S(2)}, u32[]{:S(2)}) collective-permute-start(f32[16,256]{1,0:T(8,128)S(1)} %reshape.8), channel_id=1, source_target_pairs={{0,80},{16,96},{32,112},{48,0},{64,16},{80,32},{96,48},{112,64},{1... | collective-permute-start | bytes 49160 | tf_op jit(solution)/shard_map/ppermute | solution.py:365
  56.4 1.3 copy-start.2
  73.2 32.1 %all-to-all-start.1 = ((f32[16,16,2048]{2,1,0:T(8,128)}), f32[16,16,2048]{2,1,0:T(8,128)}, u32[]{:S(2)}, u32[]{:S(2)}) async-start(f32[16,16,2048]{2,1,0:T(8,128)} %copy-done.2), calls=%async_computation.1 | async-start | bytes 4194304 | tf_op jit(solution)/shard_map/all_to_all | solution.py:357
  78.3 0.6 copy-start.6
  97.9 1.3 copy-start.3
  105.2 30.7 %copy-start = (f32[16,65536]{1,0:T(8,128)S(1)}, f32[16,65536]{1,0:T(8,128)}, u32[]{:S(2)}) copy-start(f32[16,65536]{1,0:T(8,128)} %spread.1.refs_2_) | copy-start | bytes 12582916

commit v3 on v2

--- a/solution.py
+++ b/solution.py
@@ -11,10 +11,9 @@
 
 F32 = jnp.float32
 BF16 = jnp.bfloat16
-PARTS = 2
+SHARES = (5, 3)
 TILE = 512
-GROUP = 4
-EARLY = 4
+GROUP = 8
 
 
 def fourier_tables(length):
@@ -47,7 +46,8 @@
     return freq * jnp.where(rows % 2 == 0, up, -down)
 
 
-def nodal_kernel(length, block, s_ref, g_ref, c_ref, cond_ref, cap_ref, basis_ref, forward_ref, o_ref):
+def nodal_kernel(length, block, s_ref, g_ref, c_ref, cond_ref, cap_ref, basis_ref, forward_ref, *rest):
+    o_ref = rest[-1]
     s_high, s_low = halves(s_ref[...].reshape(length, s_ref.shape[2]))
     waves = jnp.dot(
         basis_ref[...],
@@ -95,15 +95,16 @@
     o_ref[...] = (direct + derive(stored, 0, length)).reshape(o_ref.shape)
 
 
-def nodal(part, s, conductance, capacitance, block_cond, block_cap, basis, forward):
+def nodal(first, held, s, conductance, capacitance, block_cond, block_cap, basis, forward):
     count, rows, width = s.shape
     length = count * rows
     block = block_cond.shape[1]
     steps = width // TILE
     per = TILE // block
-    column = lambda i: (0, part * steps + i)
-    blocks = pl.BlockSpec((per, block, block), lambda i: (part * steps + i, 0, 0))
+    column = lambda i: (0, first + i)
+    blocks = pl.BlockSpec((per, block, block), lambda i: (first + i, 0, 0))
     table = pl.BlockSpec((length, 3 * length), lambda i: (0, 0))
+    more = [] if held is None else [held]
     return pl.pallas_call(
         functools.partial(nodal_kernel, length, block),
         grid=(steps,),
@@ -115,15 +116,17 @@
             blocks,
             table,
             table,
-        ],
-        out_specs=pl.BlockSpec((count, rows, TILE), lambda i: (0, 0, i)),
-        out_shape=jax.ShapeDtypeStruct(s.shape, F32),
+        ]
+        + [pl.BlockSpec(memory_space=pl.ANY)] * len(more),
+        out_specs=pl.BlockSpec((count, rows, TILE), lambda i: (0, 0, first + i)),
+        out_shape=jax.ShapeDtypeStruct((count, rows, conductance.shape[1]), F32),
+        input_output_aliases={7: 0} if more else {},
         compiler_params=pltpu.CompilerParams(vmem_limit_bytes=48 << 20),
         cost_estimate=pl.CostEstimate(
             flops=24 * length * length * width, transcendentals=0, bytes_accessed=20 * length * width
         ),
         name="nodal",
-    )(in_hbm(s), conductance, capacitance, block_cond, block_cap, basis, forward)
+    )(in_hbm(s), conductance, capacitance, block_cond, block_cap, basis, forward, *more)
 
 
 def pack_kernel(offset, stride, x_ref, o_ref, held, sem_in, sem_out):
@@ -146,12 +149,11 @@
         store.wait()
 
 
-def pack(x, part, count):
+def pack(x, offset, width, count):
     rows, columns = x.shape
     stride = columns // count
-    width = stride // PARTS
     return pl.pallas_call(
-        functools.partial(pack_kernel, part * width, stride),
+        functools.partial(pack_kernel, offset, stride),
         in_specs=[pl.BlockSpec(memory_space=pl.ANY)],
         out_specs=pl.BlockSpec(memory_space=pl.ANY),
         out_shape=jax.ShapeDtypeStruct((count, rows, width), F32),
@@ -274,55 +276,49 @@
     )(nodes, extra)
 
 
-def place_kernel(*refs):
-    y_refs, held_ref, o_ref = refs[:PARTS], refs[PARTS], refs[PARTS + 1]
-    y_buf, held_buf, sem_y, sem_held, sem_out = refs[PARTS + 2 :]
-    count, _, width = y_refs[0].shape
-    at = [pl.ds(t * width * PARTS, width * PARTS) for t in range(count)]
+def place_kernel(y_ref, held_ref, o_ref, y_buf, held_buf, sem_y, sem_held, sem_out):
+    count, _, stride = y_ref.shape
+    at = [pl.ds(t * stride, stride) for t in range(count)]
     loads = [
-        [pltpu.make_async_copy(held_ref.at[:, at[t]], held_buf.at[t], sem_held.at[t])]
-        + [
-            pltpu.make_async_copy(
-                y_refs[p].at[t], y_buf.at[t, :, pl.ds(p * width, width)], sem_y.at[p, t]
-            )
-            for p in range(PARTS)
-        ]
+        (
+            pltpu.make_async_copy(y_ref.at[t], y_buf.at[t], sem_y.at[t]),
+            pltpu.make_async_copy(held_ref.at[:, at[t]], held_buf.at[t], sem_held.at[t]),
+        )
         for t in range(count)
     ]
     stores = [
         pltpu.make_async_copy(y_buf.at[t], o_ref.at[:, at[t]], sem_out.at[t])
         for t in range(count)
     ]
-    for group in loads:
-        for load in group:
-            load.start()
+    for first, second in loads:
+        first.start()
+        second.start()
     for t in range(count):
-        for load in loads[t]:
-            load.wait()
+        loads[t][0].wait()
+        loads[t][1].wait()
         y_buf[t] = y_buf[t] + held_buf[t]
         stores[t].start()
     for store in stores:
         store.wait()
 
 
-def place(ys, held):
-    count, rows, width = ys[0].shape
-    whole = (count, rows, width * PARTS)
+def place(y, held):
+    count = y.shape[0]
     return pl.pallas_call(
         place_kernel,
-        in_specs=[pl.BlockSpec(memory_space=pl.ANY)] * (PARTS + 1),
+        in_specs=[pl.BlockSpec(memory_space=pl.ANY)] * 2,
         out_specs=pl.BlockSpec(memory_space=pl.ANY),
         out_shape=jax.ShapeDtypeStruct(held.shape, F32),
         scratch_shapes=[
-            pltpu.VMEM(whole, F32),
-            pltpu.VMEM(whole, F32),
-            pltpu.SemaphoreType.DMA((PARTS, count)),
+            pltpu.VMEM(y.shape, F32),
+            pltpu.VMEM(y.shape, F32),
+            pltpu.SemaphoreType.DMA((count,)),
             pltpu.SemaphoreType.DMA((count,)),
             pltpu.SemaphoreType.DMA((count,)),
         ],
         compiler_params=pltpu.CompilerParams(vmem_limit_bytes=48 << 20),
         name="place",
-    )(*[in_hbm(y) for y in ys], held)
+    )(in_hbm(y), held)
 
 
 def in_hbm(x):
@@ -356,22 +352,16 @@
     def swap(x):
         return lax.all_to_all(x, "spec", split_axis=0, concat_axis=0, tiled=True)
 
-    arrived = []
-    for part in range(PARTS):
-        packed = pack(spectrum, part, count)
-        if part == 1:
-            own_boundary = pick(spectrum, nodes, count)
-            moved = [
-                lax.ppermute(own_boundary, "dom", [(d, (d + k) % doms) for d in range(doms)])
-                for k in range(1, doms)
-            ]
-            packed, moved[:EARLY] = lax.optimization_barrier((packed, moved[:EARLY]))
-        arrived.append(swap(packed))
-
-    current = nodal(0, arrived[0], *nodal_args)
-    current, moved = lax.optimization_barrier((current, moved))
-    first = swap(current)
-
+    tiles = stride // TILE
+    early = tiles * SHARES[0] // sum(SHARES)
+    first = swap(pack(spectrum, 0, early * TILE, count))
+
+    own_boundary = pick(spectrum, nodes, count)
+    moved = [
+        lax.ppermute(own_boundary, "dom", [(d, (d + k) % doms) for d in range(doms)])
+        for k in range(1, doms)
+    ]
+    packed = pack(spectrum, early * TILE, (tiles - early) * TILE, count)
     extra = couple(
         jnp.stack(moved),
         (lax.axis_index("dom") - couple_src[0]) % doms - 1,
@@ -383,10 +373,16 @@
     )
     extra = extra.reshape(rows, count, nodes.shape[0] // count).transpose(1, 0, 2)
 
+    packed, extra, first = lax.optimization_barrier((packed, extra, first))
+    second = swap(packed)
     held = spread(extra, nodes, stride)
-    current = nodal(1, arrived[1], *nodal_args)
-    current, held = lax.optimization_barrier((current, held))
-    return place([first, swap(current)], held)
+    second, held = lax.optimization_barrier((second, held))
+
+    current = nodal(0, None, first, *nodal_args)
+    current = nodal(early, current, second, *nodal_args)
+    back = swap(current)
+
+    return place(back, held)
 
 
 def solution(mesh):

time: 141 us -> 141 us (level)
  blocking collectives: 30.7 us -> 52.4 us
  waiting for transfers between devices: 37.6 us -> 21 us
  starting transfers between devices: 25.4 us -> 19.2 us
    all_to_all x3 -> x2, waiting for transfers between devices: 37 us -> 10.8 us  [swap(): return lax.all_to_all(x, 'spec', split_axis=0, concat_axis=0, tiled=True)]
    all_to_all x1, blocking collectives: 30.7 us -> 52.4 us  [swap(): return lax.all_to_all(x, 'spec', split_axis=0, concat_axis=0, tiled=True)]
    ppermute x7, waiting for transfers between devices: 0.67 us -> 10.2 us  [shards(): lax.ppermute(own_boundary, 'dom', [(d, (d + k) % doms) for d in range(dom...]
    all_to_all x3 -> x2, starting transfers between devices: 16.9 us -> 12.8 us  [swap(): return lax.all_to_all(x, 'spec', split_axis=0, concat_axis=0, tiled=True)]
    ppermute x7, starting transfers between devices: 8.52 us -> 6.41 us  [shards(): lax.ppermute(own_boundary, 'dom', [(d, (d + k) % doms) for d in range(dom...]
    pallas_call x2, Pallas kernels: 13.3 us -> 15 us  [nodal(): pl.pallas_call(functools.partial(nodal_kernel, length, block), grid=(step...]
  transfers between devices with their start and end apart: 10 -> 9, of which waited for: 6 -> 5; matrix products, arithmetic and copies ran while one was open for 3% -> 3% of each run, Pallas kernels for 22% -> 19%
where the time goes in v3:
time: 141 us; the launch traced here: 140 us
  blocking collectives  52.4 us (37%)
  Pallas kernels  39.1 us (28%)
  waiting for transfers between devices  21 us (15%)
  starting transfers between devices  19.2 us (14%)
  local copies, waits for them, and re-layouts  6.59 us (5%)
    all_to_all x1, blocking collectives, swap(): return lax.all_to_all(x, 'spec', split_axis=0, concat_axis=0, tiled=True)  52.4 us
    pallas_call x2, Pallas kernels, nodal(): pl.pallas_call(functools.partial(nodal_kernel, length, block), grid=(step...  15 us
    all_to_all x2, starting transfers between devices, swap(): return lax.all_to_all(x, 'spec', split_axis=0, concat_axis=0, tiled=True)  12.8 us
    all_to_all x2, waiting for transfers between devices, swap(): return lax.all_to_all(x, 'spec', split_axis=0, concat_axis=0, tiled=True)  10.8 us
    ppermute x7, waiting for transfers between devices, shards(): lax.ppermute(own_boundary, 'dom', [(d, (d + k) % doms) for d in range(dom...  10.2 us
    ppermute x7, starting transfers between devices, shards(): lax.ppermute(own_boundary, 'dom', [(d, (d + k) % doms) for d in range(dom...  6.41 us
    pallas_call x1, Pallas kernels, couple(): pl.pallas_call(functools.partial(couple_kernel, length), grid_spec=pltpu....  6.38 us
    pallas_call x2, Pallas kernels, pack(): pl.pallas_call(functools.partial(pack_kernel, offset, stride), in_specs=[...  5.26 us
  transfers between devices with their start and end apart: 9, of which 5 were waited for; matrix products, arithmetic and copies ran while one was open for 3% of the time, Pallas kernels for 19%

profile of v3, /device:TPU:0, one launch (start us, length us, event | category | flops | bytes accessed | tf_op | source)
XLA Modules:
  0.0 140.3 jit_solution(1021380195016277260)
XLA Ops:
  0.0 2.8 %pack.3 = f32[16,16,2560]{2,1,0:T(8,128)} custom-call(f32[16,65536]{1,0:T(8,128)} %x_ref.5), custom_call_target="tpu_custom_call" | custom-call | tf_op jit(solution)/shard_map/pack/pallas_call | solution.py:155
  2.8 0.0 copy-start.7
  2.8 0.0 copy-start.8
  2.8 8.0 %all-to-all-start = ((f32[16,16,2560]{2,1,0:T(8,128)}), f32[16,16,2560]{2,1,0:T(8,128)}, u32[]{:S(2)}, u32[]{:S(2)}) async-start(f32[16,16,2560]{2,1,0:T(8,128)} %pack.3), calls=%async_computation | async-start | bytes 5242880 | tf_op jit(solution)/shard_map/all_to_all | solution.py:353
  10.8 0.0 copy-done.7
  10.8 0.5 fusion.2.nodes_ref
  11.4 3.9 %pick.1 = f32[16,16,128]{2,1,0:T(8,128)} custom-call(s32[256]{0:T(256)} %fusion.2.nodes_ref, f32[16,65536]{1,0:T(8,128)} %x_ref.5), custom_call_target="tpu_custom_call" | custom-call | tf_op jit(solution)/shard_map/pick/pallas_call | solution.py:187
  15.3 0.9 slice_bitcast_fusion
  16.3 0.1 reshape.8
  16.4 2.2 %collective-permute-start.6 = (f32[16,256]{1,0:T(8,128)S(1)}, f32[16,256]{1,0:T(8,128)S(1)}, u32[]{:S(2)}, u32[]{:S(2)}) collective-permute-start(f32[16,256]{1,0:T(8,128)S(1)} %reshape.8), channel_id=1, source_target_pairs={{0,112},{16,0},{32,16},{48,32},{64,48},{80,64},{96,80},{112,96},{1... | collective-permute-start | bytes 49160 | tf_op jit(solution)/shard_map/ppermute | solution.py:361
  18.6 0.9 collective-permute-start.5
  19.5 0.4 collective-permute-start.4
  19.9 2.9 %collective-permute-start.3 = (f32[16,256]{1,0:T(8,128)S(1)}, f32[16,256]{1,0:T(8,128)S(1)}, u32[]{:S(2)}, u32[]{:S(2)}) collective-permute-start(f32[16,256]{1,0:T(8,128)S(1)} %reshape.8), channel_id=1, source_target_pairs={{0,64},{16,80},{32,96},{48,112},{64,0},{80,16},{96,32},{112,48},{1... | collective-permute-start | bytes 49160 | tf_op jit(solution)/shard_map/ppermute | solution.py:361
  22.8 0.0 collective-permute-start
  23.4 0.0 copy-done.8
  23.5 0.6 pad_add_fusion.scalars_ref
  24.1 2.5 %pack.2 = f32[16,16,1536]{2,1,0:T(8,128)} custom-call(f32[16,65536]{1,0:T(8,128)} %x_ref.5), custom_call_target="tpu_custom_call" | custom-call | tf_op jit(solution)/shard_map/pack/pallas_call | solution.py:155
  26.6 0.6 collective-permute-done
  27.2 0.0 collective-permute-start.1
  27.2 4.9 %collective-permute-done.1 = f32[16,256]{1,0:T(8,128)S(1)} collective-permute-done((f32[16,256]{1,0:T(8,128)S(1)}, f32[16,256]{1,0:T(8,128)S(1)}, u32[]{:S(2)}, u32[]{:S(2)}) %collective-permute-start.1) | collective-permute-done | bytes 16416 | tf_op jit(solution)/shard_map/ppermute | solution.py:361
  32.1 0.0 collective-permute-start.2
  32.1 4.7 %collective-permute-done.2 = f32[16,256]{1,0:T(8,128)S(1)} collective-permute-done((f32[16,256]{1,0:T(8,128)S(1)}, f32[16,256]{1,0:T(8,128)S(1)}, u32[]{:S(2)}, u32[]{:S(2)}) %collective-permute-start.2) | collective-permute-done | bytes 16416 | tf_op jit(solution)/shard_map/ppermute | solution.py:361
  36.8 0.0 collective-permute-done.3
  36.8 0.0 collective-permute-done.4
  36.8 0.0 collective-permute-done.5
  36.8 0.0 collective-permute-done.6
  36.9 0.0 copy-start.6
  36.9 0.6 copy-done.6
  37.5 6.4 %couple.1 = f32[16,256]{1,0:T(8,128)} custom-call(s32[9]{0:T(128)} %pad_add_fusion.scalars_ref, f32[7,16,256]{2,1,0:T(8,128)} %copy-done.6, f32[1,7,256,256]{3,2,1,0:T(8,128)} %cond_ref.3, f32[1,7,256,256]{3,2,1,0:T(8,128)} %cap_ref.3), custom_call_target="tpu_custom_call" | custom-call | tf_op jit(solution)/shard_map/couple/pallas_call | solution.py:234
  43.9 0.0 copy-start.1
  43.9 0.0 copy-start.4
  43.9 0.0 copy-start.5
  43.9 1.0 reshape.9
  44.9 0.7 copy.18
  45.6 2.4 %all-to-all-done.s_ref = f32[16,16,2560]{2,1,0:T(8,128)} async-done(((f32[16,16,2560]{2,1,0:T(8,128)}), f32[16,16,2560]{2,1,0:T(8,128)}, u32[]{:S(2)}, u32[]{:S(2)}) %all-to-all-start) | async-done | bytes 2621472 | tf_op jit(solution)/shard_map/all_to_all | solution.py:353
  48.0 4.8 %all-to-all-start.1 = ((f32[16,16,1536]{2,1,0:T(8,128)}), f32[16,16,1536]{2,1,0:T(8,128)}, u32[]{:S(2)}, u32[]{:S(2)}) async-start(f32[16,16,1536]{2,1,0:T(8,128)} %pack.2), calls=%async_computation.1 | async-start | bytes 3145728 | tf_op jit(solution)/shard_map/all_to_all | solution.py:353
  52.8 4.6 %spread.1.held_ref = f32[16,65536]{1,0:T(8,128)} custom-call(s32[256]{0:T(256)} %fusion.2.nodes_ref, f32[16,16,16]{2,1,0:T(8,128)} %bitcast.23), custom_call_target="tpu_custom_call" | custom-call | tf_op jit(solution)/shard_map/spread/pallas_call | solution.py:266
  57.3 0.0 copy-done.1
  57.3 0.0 copy-done.4
  57.3 0.0 copy-done.5
  57.3 0.0 copy-start.2
  57.4 1.6 %copy-done.2 = f32[32,128,128]{2,1,0:T(8,128)S(1)} copy-done((f32[32,128,128]{2,1,0:T(8,128)S(1)}, f32[32,128,128]{2,1,0:T(8,128)}, u32[]{:S(2)}) %copy-start.2) | copy-done | bytes 2097176
  58.9 8.9 %nodal.2.rest_0_ = f32[16,16,4096]{2,1,0:T(8,128)} custom-call(f32[16,16,2560]{2,1,0:T(8,128)} %all-to-all-done.s_ref, f32[256,4096]{1,0:T(8,128)} %g_ref.3, f32[256,4096]{1,0:T(8,128)} %c_ref.3, f32[32,128,128]{2,1,0:T(8,128)S(1)} %copy-done.1, f32[32,128,128]{2,1,0:T(8,128)S(1)} %copy-done.2, bf16[256,768]{1,0:T(8,128)(2,1)S(1)} %copy-done.5, ...), custom_call_target="tpu_custom_call" | custom-call | flops 4026531840 | bytes 13107200 | tf_op jit(solution)/shard_map/nodal/pallas_call | solution.py:108
  67.8 8.4 %all-to-all-done.1.s_ref = f32[16,16,1536]{2,1,0:T(8,128)} async-done(((f32[16,16,1536]{2,1,0:T(8,128)}), f32[16,16,1536]{2,1,0:T(8,128)}, u32[]{:S(2)}, u32[]{:S(2)}) %all-to-all-start.1) | async-done | bytes 1572896 | tf_op jit(solution)/shard_map/all_to_all | solution.py:353
  76.2 0.0 copy-start.3
  76.2 1.6 %copy-done.3 = f32[32,128,128]{2,1,0:T(8,128)S(1)} copy-done((f32[32,128,128]{2,1,0:T(8,128)S(1)}, f32[32,128,128]{2,1,0:T(8,128)}, u32[]{:S(2)}) %copy-start.3) | copy-done | bytes 2097176
  77.8 6.1 %nodal.3 = f32[16,16,4096]{2,1,0:T(8,128)} custom-call(f32[16,16,1536]{2,1,0:T(8,128)} %all-to-all-done.1.s_ref, f32[256,4096]{1,0:T(8,128)} %g_ref.3, f32[256,4096]{1,0:T(8,128)} %c_ref.3, f32[32,128,128]{2,1,0:T(8,128)S(1)} %copy-done.1, f32[32,128,128]{2,1,0:T(8,128)S(1)} %copy-done.3, ...), custom_call_target="tpu_custom_call", output_to_operand_aliasing={{}: (7, {})} | custom-call | flops 2415919104 | bytes 7864320 | tf_op jit(solution)/shard_map/nodal/pallas_call | solution.py:108
  83.9 0.0 copy-start
  83.9 52.4 %all_to_all.15.y_ref = f32[16,16,4096]{2,1,0:T(8,128)} all-to-all(f32[16,16,4096]{2,1,0:T(8,128)} %nodal.3), channel_id=1, replica_groups=mesh['dom'=8,'spec'=16] {'spec'}, dimensions={0} | all-to-all | bytes 8388608 | tf_op jit(solution)/shard_map/all_to_all | solution.py:353
  136.3 0.0 copy-done
  136.3 4.0 %place.1 = f32[16,65536]{1,0:T(8,128)} custom-call(f32[16,16,4096]{2,1,0:T(8,128)} %all_to_all.15.y_ref, f32[16,65536]{1,0:T(8,128)S(1)} %copy-done), custom_call_target="tpu_custom_call" | custom-call | tf_op jit(solution)/shard_map/place/pallas_call | solution.py:307
  (9 shorter events, 0.1 us)
Async XLA Ops:
  2.8 8.1 %copy-start.7 = (s32[1,256]{1,0:T(1,128)S(1)}, s32[1,256]{1,0:T(1,128)}, u32[]{:S(2)}) copy-start(s32[1,256]{1,0:T(1,128)} %param.17) | copy-start | bytes 3076
  2.8 20.6 %copy-start.8 = (s32[1,7]{1,0:T(1,128)S(1)}, s32[1,7]{1,0:T(1,128)}, u32[]{:S(2)}) copy-start(s32[1,7]{1,0:T(1,128)} %param.18) | copy-start | bytes 88
  2.8 45.2 %all-to-all-start = ((f32[16,16,2560]{2,1,0:T(8,128)}), f32[16,16,2560]{2,1,0:T(8,128)}, u32[]{:S(2)}, u32[]{:S(2)}) async-start(f32[16,16,2560]{2,1,0:T(8,128)} %pack.3), calls=%async_computation | async-start | bytes 5242880 | tf_op jit(solution)/shard_map/all_to_all | solution.py:353
  16.4 20.5 %collective-permute-start.6 = (f32[16,256]{1,0:T(8,128)S(1)}, f32[16,256]{1,0:T(8,128)S(1)}, u32[]{:S(2)}, u32[]{:S(2)}) collective-permute-start(f32[16,256]{1,0:T(8,128)S(1)} %reshape.8), channel_id=1, source_target_pairs={{0,112},{16,0},{32,16},{48,32},{64,48},{80,64},{96,80},{112,96},{1... | collective-permute-start | bytes 49160 | tf_op jit(solution)/shard_map/ppermute | solution.py:361
  18.6 18.3 %collective-permute-start.5 = (f32[16,256]{1,0:T(8,128)S(1)}, f32[16,256]{1,0:T(8,128)S(1)}, u32[]{:S(2)}, u32[]{:S(2)}) collective-permute-start(f32[16,256]{1,0:T(8,128)S(1)} %reshape.8), channel_id=1, source_target_pairs={{0,96},{16,112},{32,0},{48,16},{64,32},{80,48},{96,64},{112,80},{1... | collective-permute-start | bytes 49160 | tf_op jit(solution)/shard_map/ppermute | solution.py:361
  19.5 17.3 %collective-permute-start.4 = (f32[16,256]{1,0:T(8,128)S(1)}, f32[16,256]{1,0:T(8,128)S(1)}, u32[]{:S(2)}, u32[]{:S(2)}) collective-permute-start(f32[16,256]{1,0:T(8,128)S(1)} %reshape.8), channel_id=1, source_target_pairs={{0,80},{16,96},{32,112},{48,0},{64,16},{80,32},{96,48},{112,64},{1... | collective-permute-start | bytes 49160 | tf_op jit(solution)/shard_map/ppermute | solution.py:361
  19.9 16.9 %collective-permute-start.3 = (f32[16,256]{1,0:T(8,128)S(1)}, f32[16,256]{1,0:T(8,128)S(1)}, u32[]{:S(2)}, u32[]{:S(2)}) collective-permute-start(f32[16,256]{1,0:T(8,128)S(1)} %reshape.8), channel_id=1, source_target_pairs={{0,64},{16,80},{32,96},{48,112},{64,0},{80,16},{96,32},{112,48},{1... | collective-permute-start | bytes 49160 | tf_op jit(solution)/shard_map/ppermute | solution.py:361
  22.8 4.4 %collective-permute-start = (f32[16,256]{1,0:T(8,128)S(1)}, f32[16,256]{1,0:T(8,128)S(1)}, u32[]{:S(2)}, u32[]{:S(2)}) collective-permute-start(f32[16,256]{1,0:T(8,128)S(1)} %reshape.8), channel_id=1, source_target_pairs={{0,16},{16,32},{32,48},{48,64},{64,80},{80,96},{96,112},{112,0},{1... | collective-permute-start | bytes 49160 | tf_op jit(solution)/shard_map/ppermute | solution.py:361
  27.2 4.9 %collective-permute-start.1 = (f32[16,256]{1,0:T(8,128)S(1)}, f32[16,256]{1,0:T(8,128)S(1)}, u32[]{:S(2)}, u32[]{:S(2)}) collective-permute-start(f32[16,256]{1,0:T(8,128)S(1)} %reshape.8), channel_id=1, source_target_pairs={{0,32},{16,48},{32,64},{48,80},{64,96},{80,112},{96,0},{112,16},{1... | collective-permute-start | bytes 49160 | tf_op jit(solution)/shard_map/ppermute | solution.py:361
  32.1 4.7 %collective-permute-start.2 = (f32[16,256]{1,0:T(8,128)S(1)}, f32[16,256]{1,0:T(8,128)S(1)}, u32[]{:S(2)}, u32[]{:S(2)}) collective-permute-start(f32[16,256]{1,0:T(8,128)S(1)} %reshape.8), channel_id=1, source_target_pairs={{0,48},{16,64},{32,80},{48,96},{64,112},{80,0},{96,16},{112,32},{1... | collective-permute-start | bytes 49160 | tf_op jit(solution)/shard_map/ppermute | solution.py:361
  36.9 0.7 copy-start.6
  43.9 13.5 %copy-start.1 = (f32[32,128,128]{2,1,0:T(8,128)S(1)}, f32[32,128,128]{2,1,0:T(8,128)}, u32[]{:S(2)}) copy-start(f32[32,128,128]{2,1,0:T(8,128)} %cond_ref.5) | copy-start | bytes 6291460
  43.9 13.5 %copy-start.4 = (bf16[256,768]{1,0:T(8,128)(2,1)S(1)}, bf16[256,768]{1,0:T(8,128)(2,1)}, u32[]{:S(2)}) copy-start(bf16[256,768]{1,0:T(8,128)(2,1)} %constant.54.clone.forward_ref) | copy-start | bytes 1179652
  43.9 13.5 %copy-start.5 = (bf16[256,768]{1,0:T(8,128)(2,1)S(1)}, bf16[256,768]{1,0:T(8,128)(2,1)}, u32[]{:S(2)}) copy-start(bf16[256,768]{1,0:T(8,128)(2,1)} %constant.53.clone.basis_ref) | copy-start | bytes 1179652
  48.0 28.2 %all-to-all-start.1 = ((f32[16,16,1536]{2,1,0:T(8,128)}), f32[16,16,1536]{2,1,0:T(8,128)}, u32[]{:S(2)}, u32[]{:S(2)}) async-start(f32[16,16,1536]{2,1,0:T(8,128)} %pack.2), calls=%async_computation.1 | async-start | bytes 3145728 | tf_op jit(solution)/shard_map/all_to_all | solution.py:353
  57.3 1.6 %copy-start.2 = (f32[32,128,128]{2,1,0:T(8,128)S(1)}, f32[32,128,128]{2,1,0:T(8,128)}, u32[]{:S(2)}) copy-start(f32[32,128,128]{2,1,0:T(8,128)} %cap_ref.5) | copy-start | bytes 6291460
  76.2 1.6 %copy-start.3 = (f32[32,128,128]{2,1,0:T(8,128)S(1)}, f32[32,128,128]{2,1,0:T(8,128)}, u32[]{:S(2)}) copy-start(f32[32,128,128]{2,1,0:T(8,128)} %cap_ref.5) | copy-start | bytes 6291460
  83.9 52.4 %copy-start = (f32[16,65536]{1,0:T(8,128)S(1)}, f32[16,65536]{1,0:T(8,128)}, u32[]{:S(2)}) copy-start(f32[16,65536]{1,0:T(8,128)} %spread.1.held_ref) | copy-start | bytes 12582916

commit v4 on v3

--- a/solution.py
+++ b/solution.py
@@ -12,7 +12,7 @@
 F32 = jnp.float32
 BF16 = jnp.bfloat16
 SHARES = (5, 3)
-TILE = 512
+TILE = 256
 GROUP = 8
 
 

time: 141 us -> 142 us (level)
  Pallas kernels: 39.1 us -> 42.6 us
  waiting for transfers between devices: 21 us -> 18.3 us
    pallas_call x2, Pallas kernels: 15 us -> 19.1 us  [nodal(): pl.pallas_call(functools.partial(nodal_kernel, length, block), grid=(step...]
    all_to_all x2, waiting for transfers between devices: 10.8 us -> 8.14 us  [swap(): return lax.all_to_all(x, 'spec', split_axis=0, concat_axis=0, tiled=True)]
  transfers between devices with their start and end apart: 9 -> 9, of which waited for: 5 -> 5; matrix products, arithmetic and copies ran while one was open for 3% -> 3% of each run, Pallas kernels for 19% -> 20%
where the time goes in v4:
time: 142 us; the launch traced here: 141 us
  blocking collectives  52.3 us (37%)
  Pallas kernels  42.6 us (30%)
  starting transfers between devices  18.8 us (13%)
  waiting for transfers between devices  18.3 us (13%)
  local copies, waits for them, and re-layouts  6.59 us (5%)
    all_to_all x1, blocking collectives, swap(): return lax.all_to_all(x, 'spec', split_axis=0, concat_axis=0, tiled=True)  52.3 us
    pallas_call x2, Pallas kernels, nodal(): pl.pallas_call(functools.partial(nodal_kernel, length, block), grid=(step...  19.1 us
    all_to_all x2, starting transfers between devices, swap(): return lax.all_to_all(x, 'spec', split_axis=0, concat_axis=0, tiled=True)  12.4 us
    ppermute x7, waiting for transfers between devices, shards(): lax.ppermute(own_boundary, 'dom', [(d, (d + k) % doms) for d in range(dom...  10.2 us
    all_to_all x2, waiting for transfers between devices, swap(): return lax.all_to_all(x, 'spec', split_axis=0, concat_axis=0, tiled=True)  8.14 us
    ppermute x7, starting transfers between devices, shards(): lax.ppermute(own_boundary, 'dom', [(d, (d + k) % doms) for d in range(dom...  6.41 us
    pallas_call x1, Pallas kernels, couple(): pl.pallas_call(functools.partial(couple_kernel, length), grid_spec=pltpu....  5.78 us
    pallas_call x2, Pallas kernels, pack(): pl.pallas_call(functools.partial(pack_kernel, offset, stride), in_specs=[...  5.26 us
  transfers between devices with their start and end apart: 9, of which 5 were waited for; matrix products, arithmetic and copies ran while one was open for 3% of the time, Pallas kernels for 20%

profile of v4, /device:TPU:0, one launch (start us, length us, event | category | flops | bytes accessed | tf_op | source)
XLA Modules:
  0.0 140.7 jit_solution(7316523452720023017)
XLA Ops:
  0.0 2.8 %pack.3 = f32[16,16,2560]{2,1,0:T(8,128)} custom-call(f32[16,65536]{1,0:T(8,128)} %x_ref.5), custom_call_target="tpu_custom_call" | custom-call | tf_op jit(solution)/shard_map/pack/pallas_call | solution.py:155
  2.8 0.0 copy-start.7
  2.8 0.0 copy-start.8
  2.8 8.0 %all-to-all-start = ((f32[16,16,2560]{2,1,0:T(8,128)}), f32[16,16,2560]{2,1,0:T(8,128)}, u32[]{:S(2)}, u32[]{:S(2)}) async-start(f32[16,16,2560]{2,1,0:T(8,128)} %pack.3), calls=%async_computation | async-start | bytes 5242880 | tf_op jit(solution)/shard_map/all_to_all | solution.py:353
  10.8 0.0 copy-done.7
  10.8 0.5 fusion.2.nodes_ref
  11.4 3.9 %pick.1 = f32[16,16,128]{2,1,0:T(8,128)} custom-call(s32[256]{0:T(256)} %fusion.2.nodes_ref, f32[16,65536]{1,0:T(8,128)} %x_ref.5), custom_call_target="tpu_custom_call" | custom-call | tf_op jit(solution)/shard_map/pick/pallas_call | solution.py:187
  15.3 0.9 slice_bitcast_fusion
  16.3 0.1 reshape.8
  16.4 2.2 %collective-permute-start.6 = (f32[16,256]{1,0:T(8,128)S(1)}, f32[16,256]{1,0:T(8,128)S(1)}, u32[]{:S(2)}, u32[]{:S(2)}) collective-permute-start(f32[16,256]{1,0:T(8,128)S(1)} %reshape.8), channel_id=1, source_target_pairs={{0,112},{16,0},{32,16},{48,32},{64,48},{80,64},{96,80},{112,96},{1... | collective-permute-start | bytes 49160 | tf_op jit(solution)/shard_map/ppermute | solution.py:361
  18.6 0.9 collective-permute-start.5
  19.5 0.4 collective-permute-start.4
  19.9 2.9 %collective-permute-start.3 = (f32[16,256]{1,0:T(8,128)S(1)}, f32[16,256]{1,0:T(8,128)S(1)}, u32[]{:S(2)}, u32[]{:S(2)}) collective-permute-start(f32[16,256]{1,0:T(8,128)S(1)} %reshape.8), channel_id=1, source_target_pairs={{0,64},{16,80},{32,96},{48,112},{64,0},{80,16},{96,32},{112,48},{1... | collective-permute-start | bytes 49160 | tf_op jit(solution)/shard_map/ppermute | solution.py:361
  22.8 0.0 collective-permute-start
  23.4 0.0 copy-done.8
  23.5 0.6 pad_add_fusion.scalars_ref
  24.1 2.5 %pack.2 = f32[16,16,1536]{2,1,0:T(8,128)} custom-call(f32[16,65536]{1,0:T(8,128)} %x_ref.5), custom_call_target="tpu_custom_call" | custom-call | tf_op jit(solution)/shard_map/pack/pallas_call | solution.py:155
  26.6 0.6 collective-permute-done
  27.2 0.0 collective-permute-start.1
  27.2 4.9 %collective-permute-done.1 = f32[16,256]{1,0:T(8,128)S(1)} collective-permute-done((f32[16,256]{1,0:T(8,128)S(1)}, f32[16,256]{1,0:T(8,128)S(1)}, u32[]{:S(2)}, u32[]{:S(2)}) %collective-permute-start.1) | collective-permute-done | bytes 16416 | tf_op jit(solution)/shard_map/ppermute | solution.py:361
  32.1 0.0 collective-permute-start.2
  32.1 4.7 %collective-permute-done.2 = f32[16,256]{1,0:T(8,128)S(1)} collective-permute-done((f32[16,256]{1,0:T(8,128)S(1)}, f32[16,256]{1,0:T(8,128)S(1)}, u32[]{:S(2)}, u32[]{:S(2)}) %collective-permute-start.2) | collective-permute-done | bytes 16416 | tf_op jit(solution)/shard_map/ppermute | solution.py:361
  36.8 0.0 collective-permute-done.3
  36.8 0.0 collective-permute-done.4
  36.8 0.0 collective-permute-done.5
  36.8 0.0 collective-permute-done.6
  36.9 0.0 copy-start.6
  36.9 0.6 copy-done.6
  37.5 5.8 %couple.1 = f32[16,256]{1,0:T(8,128)} custom-call(s32[9]{0:T(128)} %pad_add_fusion.scalars_ref, f32[7,16,256]{2,1,0:T(8,128)} %copy-done.6, f32[1,7,256,256]{3,2,1,0:T(8,128)} %cond_ref.3, f32[1,7,256,256]{3,2,1,0:T(8,128)} %cap_ref.3), custom_call_target="tpu_custom_call" | custom-call | tf_op jit(solution)/shard_map/couple/pallas_call | solution.py:234
  43.3 0.0 copy-start.1
  43.3 0.0 copy-start.4
  43.3 0.0 copy-start.5
  43.3 1.0 reshape.9
  44.3 0.7 copy.18
  45.0 3.0 %all-to-all-done.s_ref = f32[16,16,2560]{2,1,0:T(8,128)} async-done(((f32[16,16,2560]{2,1,0:T(8,128)}), f32[16,16,2560]{2,1,0:T(8,128)}, u32[]{:S(2)}, u32[]{:S(2)}) %all-to-all-start) | async-done | bytes 2621472 | tf_op jit(solution)/shard_map/all_to_all | solution.py:353
  48.0 4.4 %all-to-all-start.1 = ((f32[16,16,1536]{2,1,0:T(8,128)}), f32[16,16,1536]{2,1,0:T(8,128)}, u32[]{:S(2)}, u32[]{:S(2)}) async-start(f32[16,16,1536]{2,1,0:T(8,128)} %pack.2), calls=%async_computation.1 | async-start | bytes 3145728 | tf_op jit(solution)/shard_map/all_to_all | solution.py:353
  52.4 4.6 %spread.1.held_ref = f32[16,65536]{1,0:T(8,128)} custom-call(s32[256]{0:T(256)} %fusion.2.nodes_ref, f32[16,16,16]{2,1,0:T(8,128)} %bitcast.23), custom_call_target="tpu_custom_call" | custom-call | tf_op jit(solution)/shard_map/spread/pallas_call | solution.py:266
  56.9 0.0 copy-done.1
  56.9 0.0 copy-done.4
  56.9 0.0 copy-done.5
  56.9 0.0 copy-start.2
  57.0 1.6 %copy-done.2 = f32[32,128,128]{2,1,0:T(8,128)S(1)} copy-done((f32[32,128,128]{2,1,0:T(8,128)S(1)}, f32[32,128,128]{2,1,0:T(8,128)}, u32[]{:S(2)}) %copy-start.2) | copy-done | bytes 2097176
  58.5 11.6 %nodal.2.rest_0_ = f32[16,16,4096]{2,1,0:T(8,128)} custom-call(f32[16,16,2560]{2,1,0:T(8,128)} %all-to-all-done.s_ref, f32[256,4096]{1,0:T(8,128)} %g_ref.3, f32[256,4096]{1,0:T(8,128)} %c_ref.3, f32[32,128,128]{2,1,0:T(8,128)S(1)} %copy-done.1, f32[32,128,128]{2,1,0:T(8,128)S(1)} %copy-done.2, bf16[256,768]{1,0:T(8,128)(2,1)S(1)} %copy-done.5, ...), custom_call_target="tpu_custom_call" | custom-call | flops 4026531840 | bytes 13107200 | tf_op jit(solution)/shard_map/nodal/pallas_call | solution.py:108
  70.1 5.1 %all-to-all-done.1.s_ref = f32[16,16,1536]{2,1,0:T(8,128)} async-done(((f32[16,16,1536]{2,1,0:T(8,128)}), f32[16,16,1536]{2,1,0:T(8,128)}, u32[]{:S(2)}, u32[]{:S(2)}) %all-to-all-start.1) | async-done | bytes 1572896 | tf_op jit(solution)/shard_map/all_to_all | solution.py:353
  75.3 0.0 copy-start.3
  75.3 1.6 %copy-done.3 = f32[32,128,128]{2,1,0:T(8,128)S(1)} copy-done((f32[32,128,128]{2,1,0:T(8,128)S(1)}, f32[32,128,128]{2,1,0:T(8,128)}, u32[]{:S(2)}) %copy-start.3) | copy-done | bytes 2097176
  76.9 7.5 %nodal.3 = f32[16,16,4096]{2,1,0:T(8,128)} custom-call(f32[16,16,1536]{2,1,0:T(8,128)} %all-to-all-done.1.s_ref, f32[256,4096]{1,0:T(8,128)} %g_ref.3, f32[256,4096]{1,0:T(8,128)} %c_ref.3, f32[32,128,128]{2,1,0:T(8,128)S(1)} %copy-done.1, f32[32,128,128]{2,1,0:T(8,128)S(1)} %copy-done.3, ...), custom_call_target="tpu_custom_call", output_to_operand_aliasing={{}: (7, {})} | custom-call | flops 2415919104 | bytes 7864320 | tf_op jit(solution)/shard_map/nodal/pallas_call | solution.py:108
  84.4 0.0 copy-start
  84.4 52.3 %all_to_all.15.y_ref = f32[16,16,4096]{2,1,0:T(8,128)} all-to-all(f32[16,16,4096]{2,1,0:T(8,128)} %nodal.3), channel_id=1, replica_groups=mesh['dom'=8,'spec'=16] {'spec'}, dimensions={0} | all-to-all | bytes 8388608 | tf_op jit(solution)/shard_map/all_to_all | solution.py:353
  136.7 0.0 copy-done
  136.7 4.0 %place.1 = f32[16,65536]{1,0:T(8,128)} custom-call(f32[16,16,4096]{2,1,0:T(8,128)} %all_to_all.15.y_ref, f32[16,65536]{1,0:T(8,128)S(1)} %copy-done), custom_call_target="tpu_custom_call" | custom-call | tf_op jit(solution)/shard_map/place/pallas_call | solution.py:307
  (9 shorter events, 0.1 us)
Async XLA Ops:
  2.8 8.1 %copy-start.7 = (s32[1,256]{1,0:T(1,128)S(1)}, s32[1,256]{1,0:T(1,128)}, u32[]{:S(2)}) copy-start(s32[1,256]{1,0:T(1,128)} %param.17) | copy-start | bytes 3076
  2.8 20.6 %copy-start.8 = (s32[1,7]{1,0:T(1,128)S(1)}, s32[1,7]{1,0:T(1,128)}, u32[]{:S(2)}) copy-start(s32[1,7]{1,0:T(1,128)} %param.18) | copy-start | bytes 88
  2.8 45.2 %all-to-all-start = ((f32[16,16,2560]{2,1,0:T(8,128)}), f32[16,16,2560]{2,1,0:T(8,128)}, u32[]{:S(2)}, u32[]{:S(2)}) async-start(f32[16,16,2560]{2,1,0:T(8,128)} %pack.3), calls=%async_computation | async-start | bytes 5242880 | tf_op jit(solution)/shard_map/all_to_all | solution.py:353
  16.4 20.5 %collective-permute-start.6 = (f32[16,256]{1,0:T(8,128)S(1)}, f32[16,256]{1,0:T(8,128)S(1)}, u32[]{:S(2)}, u32[]{:S(2)}) collective-permute-start(f32[16,256]{1,0:T(8,128)S(1)} %reshape.8), channel_id=1, source_target_pairs={{0,112},{16,0},{32,16},{48,32},{64,48},{80,64},{96,80},{112,96},{1... | collective-permute-start | bytes 49160 | tf_op jit(solution)/shard_map/ppermute | solution.py:361
  18.6 18.3 %collective-permute-start.5 = (f32[16,256]{1,0:T(8,128)S(1)}, f32[16,256]{1,0:T(8,128)S(1)}, u32[]{:S(2)}, u32[]{:S(2)}) collective-permute-start(f32[16,256]{1,0:T(8,128)S(1)} %reshape.8), channel_id=1, source_target_pairs={{0,96},{16,112},{32,0},{48,16},{64,32},{80,48},{96,64},{112,80},{1... | collective-permute-start | bytes 49160 | tf_op jit(solution)/shard_map/ppermute | solution.py:361
  19.5 17.3 %collective-permute-start.4 = (f32[16,256]{1,0:T(8,128)S(1)}, f32[16,256]{1,0:T(8,128)S(1)}, u32[]{:S(2)}, u32[]{:S(2)}) collective-permute-start(f32[16,256]{1,0:T(8,128)S(1)} %reshape.8), channel_id=1, source_target_pairs={{0,80},{16,96},{32,112},{48,0},{64,16},{80,32},{96,48},{112,64},{1... | collective-permute-start | bytes 49160 | tf_op jit(solution)/shard_map/ppermute | solution.py:361
  19.9 16.9 %collective-permute-start.3 = (f32[16,256]{1,0:T(8,128)S(1)}, f32[16,256]{1,0:T(8,128)S(1)}, u32[]{:S(2)}, u32[]{:S(2)}) collective-permute-start(f32[16,256]{1,0:T(8,128)S(1)} %reshape.8), channel_id=1, source_target_pairs={{0,64},{16,80},{32,96},{48,112},{64,0},{80,16},{96,32},{112,48},{1... | collective-permute-start | bytes 49160 | tf_op jit(solution)/shard_map/ppermute | solution.py:361
  22.8 4.4 %collective-permute-start = (f32[16,256]{1,0:T(8,128)S(1)}, f32[16,256]{1,0:T(8,128)S(1)}, u32[]{:S(2)}, u32[]{:S(2)}) collective-permute-start(f32[16,256]{1,0:T(8,128)S(1)} %reshape.8), channel_id=1, source_target_pairs={{0,16},{16,32},{32,48},{48,64},{64,80},{80,96},{96,112},{112,0},{1... | collective-permute-start | bytes 49160 | tf_op jit(solution)/shard_map/ppermute | solution.py:361
  27.2 4.9 %collective-permute-start.1 = (f32[16,256]{1,0:T(8,128)S(1)}, f32[16,256]{1,0:T(8,128)S(1)}, u32[]{:S(2)}, u32[]{:S(2)}) collective-permute-start(f32[16,256]{1,0:T(8,128)S(1)} %reshape.8), channel_id=1, source_target_pairs={{0,32},{16,48},{32,64},{48,80},{64,96},{80,112},{96,0},{112,16},{1... | collective-permute-start | bytes 49160 | tf_op jit(solution)/shard_map/ppermute | solution.py:361
  32.1 4.7 %collective-permute-start.2 = (f32[16,256]{1,0:T(8,128)S(1)}, f32[16,256]{1,0:T(8,128)S(1)}, u32[]{:S(2)}, u32[]{:S(2)}) collective-permute-start(f32[16,256]{1,0:T(8,128)S(1)} %reshape.8), channel_id=1, source_target_pairs={{0,48},{16,64},{32,80},{48,96},{64,112},{80,0},{96,16},{112,32},{1... | collective-permute-start | bytes 49160 | tf_op jit(solution)/shard_map/ppermute | solution.py:361
  36.9 0.7 copy-start.6
  43.3 13.6 %copy-start.1 = (f32[32,128,128]{2,1,0:T(8,128)S(1)}, f32[32,128,128]{2,1,0:T(8,128)}, u32[]{:S(2)}) copy-start(f32[32,128,128]{2,1,0:T(8,128)} %cond_ref.5) | copy-start | bytes 6291460
  43.3 13.6 %copy-start.4 = (bf16[256,768]{1,0:T(8,128)(2,1)S(1)}, bf16[256,768]{1,0:T(8,128)(2,1)}, u32[]{:S(2)}) copy-start(bf16[256,768]{1,0:T(8,128)(2,1)} %constant.54.clone.forward_ref) | copy-start | bytes 1179652
  43.3 13.6 %copy-start.5 = (bf16[256,768]{1,0:T(8,128)(2,1)S(1)}, bf16[256,768]{1,0:T(8,128)(2,1)}, u32[]{:S(2)}) copy-start(bf16[256,768]{1,0:T(8,128)(2,1)} %constant.53.clone.basis_ref) | copy-start | bytes 1179652
  48.0 27.3 %all-to-all-start.1 = ((f32[16,16,1536]{2,1,0:T(8,128)}), f32[16,16,1536]{2,1,0:T(8,128)}, u32[]{:S(2)}, u32[]{:S(2)}) async-start(f32[16,16,1536]{2,1,0:T(8,128)} %pack.2), calls=%async_computation.1 | async-start | bytes 3145728 | tf_op jit(solution)/shard_map/all_to_all | solution.py:353
  56.9 1.6 %copy-start.2 = (f32[32,128,128]{2,1,0:T(8,128)S(1)}, f32[32,128,128]{2,1,0:T(8,128)}, u32[]{:S(2)}) copy-start(f32[32,128,128]{2,1,0:T(8,128)} %cap_ref.5) | copy-start | bytes 6291460
  75.3 1.6 %copy-start.3 = (f32[32,128,128]{2,1,0:T(8,128)S(1)}, f32[32,128,128]{2,1,0:T(8,128)}, u32[]{:S(2)}) copy-start(f32[32,128,128]{2,1,0:T(8,128)} %cap_ref.5) | copy-start | bytes 6291460
  84.4 52.3 %copy-start = (f32[16,65536]{1,0:T(8,128)S(1)}, f32[16,65536]{1,0:T(8,128)}, u32[]{:S(2)}) copy-start(f32[16,65536]{1,0:T(8,128)} %spread.1.held_ref) | copy-start | bytes 12582916
